TPU v7x, 32 devices: a whole 2x2x4 slice. The times are simulated.
32 devices in a mesh: tm: 8 (over z, y), opt: 4 (over x, core).
Axes of the slice: x: 2, y: 2, z: 4, core: 2. Of those that a mesh axis runs over, the one named last changes fastest.
Arguments:
- wave: float32 [8, 8, 4160], P('opt', 'tm'), may hold values from -6 to 6
- crop_offsets: int32 [8], P('opt'), may hold values from 0 to 64, as said below
- squeeze_order: int32 [8], replicated, may hold values from 0 to 7, each once
- mel: bfloat16 [8, 128, 80], P('opt', 'tm'), may hold values from -6 to 6
- mel_index: int32 [8, 4096, 8], P('opt', 'tm'), may hold values from 0 to 15, as said below
- soap_slots: int32 [12], replicated, may hold values from 0 to 11, each once
- step_count: int32 [1], replicated, may hold values from 2 to 20
- in_weight: float32 [12, 512, 512], P('opt'), may hold values from -0.15625 to 0.15625
- soap_first: float32 [12, 512, 512], P('opt'), may hold values from -9.1552734e-05 to 9.1552734e-05
- soap_second: float32 [12, 512, 512], P('opt'), may hold values from 1.5258789e-09 to 2.4414062e-08
- left_stats: float32 [12, 512, 512], P('opt'), as said below
- right_stats: float32 [12, 512, 512], P('opt'), as said below
- left_basis: float32 [12, 512, 512], P('opt')
- right_basis: float32 [12, 512, 512], P('opt')
- cond_weight: float32 [2048, 640], P('tm', 'opt'), may hold values from -0.25 to 0.25
- cond_first: float32 [2048, 640], P('tm', 'opt'), may hold values from -9.1552734e-05 to 9.1552734e-05
- cond_second: float32 [2048, 640], P('tm', 'opt'), may hold values from 1.5258789e-09 to 2.4414062e-08
- out_weight: float32 [3, 512, 512], P(None, 'tm', 'opt'), may hold values from -0.25 to 0.25
- out_first: float32 [3, 512, 512], P(None, 'tm', 'opt'), may hold values from -9.1552734e-05 to 9.1552734e-05
- out_second: float32 [3, 512, 512], P(None, 'tm', 'opt'), may hold values from 1.5258789e-09 to 2.4414062e-08
- aux_params: float32 [17, 512], replicated
- aux_first: float32 [17, 512], replicated
- aux_second: float32 [17, 512], replicated
- flow_params: float32 [6, 7], replicated
- flow_first: float32 [6, 7], replicated, may hold values from -0.15625 to 0.15625
- flow_second: float32 [6, 7], replicated, may hold values from 1e-05 to 0.001
Outputs:
- loss: float32 [], replicated
- in_new: float32 [12, 512, 512], P('opt')
- soap_first_new: float32 [12, 512, 512], P('opt')
- soap_second_new: float32 [12, 512, 512], P('opt')
- left_stats_new: float32 [12, 512, 512], P('opt')
- right_stats_new: float32 [12, 512, 512], P('opt')
- left_basis_new: float32 [12, 512, 512], P('opt')
- right_basis_new: float32 [12, 512, 512], P('opt')
- cond_new: float32 [2048, 640], P('tm', 'opt')
- cond_first_new: float32 [2048, 640], P('tm', 'opt')
- cond_second_new: float32 [2048, 640], P('tm', 'opt')
- out_new: float32 [3, 512, 512], P(None, 'tm', 'opt')
- out_first_new: float32 [3, 512, 512], P(None, 'tm', 'opt')
- out_second_new: float32 [3, 512, 512], P(None, 'tm', 'opt')
- aux_new: float32 [17, 512], replicated
- aux_first_new: float32 [17, 512], replicated
- aux_second_new: float32 [17, 512], replicated
- flow_new: float32 [6, 7], replicated
- flow_first_new: float32 [6, 7], replicated
- flow_second_new: float32 [6, 7], replicated
Inputs may be any that keep to these rules, and one draw needn't show every extreme that they name: `crop_offsets`: 0 and 64 both occur. `mel_index`: counted within the 16 frames of the same block of 512 groups. `soap_slots`: each slot number once. `squeeze_order`: each sample once. `left_stats`: symmetric positive definite. `right_stats`: symmetric positive definite.
All inputs are finite; a program needn't handle non-finite values.
Results may differ from a plain program's by a relative error of at most 0.0065.
Values may be sent and summed in bfloat16 or wider, within the bound.
No kernel may reach another device: no remote copies, remote signals or barrier semaphores. Data moves between devices by JAX's collectives and lax.ppermute only.
A program may use at most 192 MiB of HBM per device.

v0:
```python
import jax
import jax.numpy as jnp
from jax import lax
from jax.sharding import PartitionSpec as P

H = 512
MEL = 80
LAYERS = 2
FIRST_DILATION = 64
G_DEV = 512
FR_DEV = 16
NMAT = 12


highest = lax.Precision.HIGHEST
beta_first = 0.9
beta_second = 0.99
beta_stats = 0.95
learn_rate = 0.02
aux_rate = 0.15
epsilon = 1e-08
decay_weight = 0.01
early_weight = 0.5


def with_halo(cells, sides, width):
    for axis, dim in sides:
        count = lax.axis_size(axis)
        ends = count - 1
        head = lax.slice_in_dim(cells, 0, width, axis=dim)
        tail = lax.slice_in_dim(cells, cells.shape[dim] - width, cells.shape[dim], axis=dim)
        cells = jnp.concatenate(
            [
                lax.ppermute(tail, axis, [(i, (i + 1) % count) for i in range(ends)]),
                cells,
                lax.ppermute(head, axis, [((i + 1) % count, i) for i in range(ends)]),
            ],
            axis=dim,
        )
    return cells


def full_dot(matrix_a, matrix_b):
    return jnp.dot(matrix_a, matrix_b, precision=highest, preferred_element_type=jnp.float32)


def half_dot(matrix_a, matrix_b):
    return jnp.dot(matrix_a, matrix_b, preferred_element_type=jnp.float32)


def rows_dot(matrix_a, matrix_b, exactness=None):
    return lax.dot_general(
        matrix_a,
        matrix_b,
        (((0,), (0,)), ((), ())),
        precision=exactness,
        preferred_element_type=jnp.float32,
    )


def cols_dot(matrix_a, matrix_b):
    return lax.dot_general(
        matrix_a, matrix_b, (((1,), (1,)), ((), ())), preferred_element_type=jnp.float32
    )


def orthonormal(matrix):
    factor = jnp.linalg.cholesky(full_dot(matrix.T, matrix))
    return jax.scipy.linalg.solve_triangular(factor, matrix.T, lower=True).T


def soap_update(
    weight,
    gradient,
    moment_one,
    moment_two,
    left_stats,
    right_stats,
    left_basis,
    right_basis,
    steps_done,
):
    rotated = full_dot(full_dot(left_basis.T, gradient), right_basis)
    moment_one = beta_first * moment_one + (1.0 - beta_first) * rotated
    moment_two = beta_second * moment_two + (1.0 - beta_second) * rotated * rotated
    direction = (
        moment_one
        / (1.0 - beta_first**steps_done)
        / (jnp.sqrt(moment_two / (1.0 - beta_second**steps_done)) + epsilon)
    )
    weight = weight - learn_rate * (
        full_dot(full_dot(left_basis, direction), right_basis.T) + decay_weight * weight
    )
    left_stats = beta_stats * left_stats + (1.0 - beta_stats) * full_dot(gradient, gradient.T)
    right_stats = beta_stats * right_stats + (1.0 - beta_stats) * full_dot(gradient.T, gradient)
    left_new = orthonormal(full_dot(left_stats, left_basis))
    right_new = orthonormal(full_dot(right_stats, right_basis))
    initial = full_dot(full_dot(left_basis, moment_one), right_basis.T)
    moment_one = full_dot(full_dot(left_new.T, initial), right_new)
    return (weight, moment_one, moment_two, left_stats, right_stats, left_new, right_new)


def adamw_update(weight, gradient, moment_one, moment_two, steps_done, rate_value):
    moment_one = beta_first * moment_one + (1.0 - beta_first) * gradient
    moment_two = beta_second * moment_two + (1.0 - beta_second) * gradient * gradient
    direction = (
        moment_one
        / (1.0 - beta_first**steps_done)
        / (jnp.sqrt(moment_two / (1.0 - beta_second**steps_done)) + epsilon)
    )
    weight = weight - rate_value * (direction + decay_weight * weight)
    return (weight, moment_one, moment_two)


def gate_parts(before_gate):
    half_width = before_gate.shape[1] // 2
    return (jnp.tanh(before_gate[:, :half_width]), jax.nn.sigmoid(before_gate[:, half_width:]))


def layer_forward(
    hidden_state, conditioning_part, bias_vector_row, taps, dilation_step, crops_current
):
    row_count, channels = hidden_state.shape
    length = row_count // crops_current
    hidden_low = hidden_state.astype(jnp.bfloat16).reshape(crops_current, length, channels)
    padded_input = with_halo(hidden_low, (("tm", 1),), dilation_step)
    before_gate = conditioning_part + bias_vector_row
    for k in range(3):
        window = padded_input[:, k * dilation_step : k * dilation_step + length].reshape(
            row_count, channels
        )
        before_gate = before_gate + half_dot(window, taps[k])
    tangent, sigmoid_part = gate_parts(before_gate)
    gated = (tangent * sigmoid_part).astype(jnp.bfloat16)
    return (padded_input, before_gate, gated)


def layer_backward(padded_input, before_gate, taps, gated_gradient, dilation_step):
    crops_current, width_all, channels = padded_input.shape
    length = width_all - 2 * dilation_step
    row_count = crops_current * length
    tangent, sigmoid_part = gate_parts(before_gate)
    grad_before = jnp.concatenate(
        [
            gated_gradient * (1.0 - tangent * tangent) * sigmoid_part,
            gated_gradient * tangent * sigmoid_part * (1.0 - sigmoid_part),
        ],
        axis=1,
    ).astype(jnp.bfloat16)
    tap_grads = []
    grad_padded = jnp.zeros((crops_current, width_all, channels), jnp.float32)
    for k in range(3):
        window = padded_input[:, k * dilation_step : k * dilation_step + length].reshape(
            row_count, channels
        )
        tap_grads.append(rows_dot(window, grad_before))
        flowing = cols_dot(grad_before, taps[k]).reshape(crops_current, length, channels)
        grad_padded = grad_padded.at[:, k * dilation_step : k * dilation_step + length].add(flowing)
    rims = jnp.concatenate(
        [grad_padded[:, :dilation_step], grad_padded[:, length + dilation_step :]], axis=1
    )
    extended = with_halo(rims, (("tm", 1),), dilation_step)
    core = grad_padded[:, dilation_step : dilation_step + length]
    core = core.at[:, :dilation_step].add(extended[:, :dilation_step])
    core = core.at[:, length - dilation_step :].add(extended[:, 3 * dilation_step :])
    return (grad_before, jnp.stack(tap_grads), core.reshape(row_count, channels))


def shards(
    wave,
    crop_offsets,
    squeeze_order,
    mel,
    mel_index,
    soap_slots,
    step_count,
    in_weight,
    soap_first,
    soap_second,
    left_stats,
    right_stats,
    left_basis,
    right_basis,
    cond_weight,
    cond_first,
    cond_second,
    out_weight,
    out_first,
    out_second,
    aux_params,
    aux_first,
    aux_second,
    flow_params,
    flow_first,
    flow_second,
):
    crops_current = wave.shape[0]
    row_count = crops_current * G_DEV
    tokens_all = row_count * lax.axis_size("tm") * lax.axis_size("opt")
    scale_final = 1.0 / (6.0 * tokens_all)
    scale_early = early_weight / (2.0 * tokens_all)
    steps_done = step_count[0].astype(jnp.float32)
    owned = NMAT // lax.axis_size("opt")
    slot_weights = lax.all_gather(in_weight.astype(jnp.bfloat16), "opt", axis=0, tiled=True)
    matrices = jnp.take(slot_weights, jnp.argsort(soap_slots), axis=0)
    every_tap_weight = jnp.transpose(matrices.reshape(LAYERS, 3, 2, H, H), (0, 1, 3, 2, 4)).reshape(
        LAYERS, 3, H, 2 * H
    )
    cond_cols, out_cols = (
        lax.all_gather(cond_weight.astype(jnp.bfloat16), "opt", axis=1, tiled=True),
        lax.all_gather(out_weight.astype(jnp.bfloat16), "opt", axis=2, tiled=True),
    )
    cond_full, out_full = (
        lax.all_gather(cond_cols, "tm", axis=0, tiled=True),
        lax.all_gather(out_cols, "tm", axis=1, tiled=True),
    )

    def squeeze_one(samples, offset):
        segment = lax.dynamic_slice_in_dim(samples, offset, 8 * G_DEV, 0)
        return jnp.take(segment.reshape(G_DEV, 8), squeeze_order, axis=1)

    squeezed = jax.vmap(squeeze_one)(wave[:, 0], crop_offsets).reshape(row_count, 8)
    frames_hit = (mel_index[..., None] == jnp.arange(FR_DEV, dtype=jnp.int32)).astype(jnp.bfloat16)
    conditioning = (
        jnp.einsum("cgjf,cfm->cgjm", frames_hit, mel, preferred_element_type=jnp.float32)
        .astype(jnp.bfloat16)
        .reshape(row_count, 8 * MEL)
    )
    spectral = cols_dot(conditioning, cond_full)
    flow_matrix = flow_params[:, :6]
    mixed = full_dot(squeezed[:, 2:], flow_matrix.T)
    lower_half = mixed[:, :3]
    upper_half = mixed[:, 3:]
    hidden_state = full_dot(lower_half, aux_params[0:3]) + aux_params[3]
    skip_total = jnp.zeros((row_count, H), jnp.float32)
    bias_base = 4 + 2 * LAYERS
    saved = []
    for layer_number in range(LAYERS):
        bias_vector_row = aux_params[4 + 2 * layer_number : 6 + 2 * layer_number].reshape(2 * H)
        conditioning_part = spectral[:, 2 * H * layer_number : 2 * H * (layer_number + 1)]
        padded_input, before_gate, gated = layer_forward(
            hidden_state,
            conditioning_part,
            bias_vector_row,
            every_tap_weight[layer_number],
            FIRST_DILATION * 2**layer_number,
            crops_current,
        )
        if layer_number < LAYERS - 1:
            hidden_state = (
                hidden_state
                + half_dot(gated, out_full[layer_number])
                + aux_params[bias_base + layer_number]
            )
        skip_total = (
            skip_total
            + half_dot(gated, out_full[LAYERS - 1 + layer_number])
            + aux_params[bias_base + LAYERS - 1 + layer_number]
        )
        saved.append((padded_input, before_gate, gated))
    end_weight = aux_params[4 * LAYERS + 3 :]
    outputs = full_dot(skip_total, end_weight.T) + flow_params[:, 6]
    log_scale = outputs[:, :3]
    growth = jnp.exp(log_scale)
    z_upper = growth * upper_half + outputs[:, 3:]
    final_part = (
        0.5 * jnp.sum(lower_half * lower_half)
        + 0.5 * jnp.sum(z_upper * z_upper)
        - jnp.sum(log_scale)
    )
    early_part = 0.5 * jnp.sum(squeezed[:, :2] * squeezed[:, :2])
    grad_upper_z = scale_final * z_upper
    grad_outputs = jnp.concatenate(
        [grad_upper_z * growth * upper_half - scale_final, grad_upper_z], axis=1
    )
    grad_upper = grad_upper_z * growth
    grad_end = rows_dot(grad_outputs, skip_total, highest)
    grad_end_bias = jnp.sum(grad_outputs, axis=0)
    grad_skip = full_dot(grad_outputs, end_weight).astype(jnp.bfloat16)
    grad_hidden = jnp.zeros((row_count, H), jnp.float32)
    out_grads = [None] * (2 * LAYERS - 1)
    out_bias_grads = [None] * (2 * LAYERS - 1)
    in_bias_grads = [None] * LAYERS
    tap_grads = [None] * LAYERS
    spectral_grads = [None] * LAYERS
    for layer_number in reversed(range(LAYERS)):
        padded_input, before_gate, gated = saved[layer_number]
        skip_index = LAYERS - 1 + layer_number
        gated_gradient = cols_dot(grad_skip, out_full[skip_index])
        out_grads[skip_index] = rows_dot(gated, grad_skip)
        out_bias_grads[skip_index] = jnp.sum(grad_skip.astype(jnp.float32), axis=0)
        if layer_number < LAYERS - 1:
            grad_residual = grad_hidden.astype(jnp.bfloat16)
            gated_gradient = gated_gradient + cols_dot(grad_residual, out_full[layer_number])
            out_grads[layer_number] = rows_dot(gated, grad_residual)
            out_bias_grads[layer_number] = jnp.sum(grad_residual.astype(jnp.float32), axis=0)
        grad_before, tap_grads[layer_number], grad_conv = layer_backward(
            padded_input,
            before_gate,
            every_tap_weight[layer_number],
            gated_gradient,
            FIRST_DILATION * 2**layer_number,
        )
        in_bias_grads[layer_number] = jnp.sum(grad_before.astype(jnp.float32), axis=0)
        spectral_grads[layer_number] = grad_before
        grad_hidden = grad_hidden + grad_conv
    grad_start = rows_dot(lower_half, grad_hidden, highest)
    grad_start_bias = jnp.sum(grad_hidden, axis=0)
    grad_lower = scale_final * lower_half + full_dot(grad_hidden, aux_params[0:3].T)
    grad_mixed = jnp.concatenate([grad_lower, grad_upper], axis=1)
    grad_flow = jnp.concatenate(
        [rows_dot(grad_mixed, squeezed[:, 2:], highest), grad_end_bias[:, None]], axis=1
    )
    grad_aux = jnp.concatenate(
        [
            grad_start,
            grad_start_bias[None],
            jnp.stack(in_bias_grads).reshape(2 * LAYERS, H),
            jnp.stack(out_bias_grads),
            grad_end,
        ],
        axis=0,
    )
    parts, grad_aux, grad_flow = lax.psum(
        (jnp.stack([final_part, early_part]), grad_aux, grad_flow), ("tm", "opt")
    )
    factor = jnp.linalg.cholesky(full_dot(flow_matrix, flow_matrix.T))
    log_det = jnp.sum(jnp.log(jnp.diagonal(factor)))
    inverse_t = jax.scipy.linalg.cho_solve((factor, True), flow_matrix)
    grad_flow = grad_flow.at[:, :6].add(-inverse_t / 6.0)
    loss = parts[0] * scale_final + parts[1] * scale_early - log_det / 6.0
    grad_cond = rows_dot(jnp.concatenate(spectral_grads, axis=1), conditioning)
    grad_cond, grad_out = (
        lax.psum_scatter(grad_cond, "tm", scatter_dimension=0, tiled=True),
        lax.psum_scatter(jnp.stack(out_grads), "tm", scatter_dimension=1, tiled=True),
    )
    grad_cond, grad_out = (
        lax.psum_scatter(grad_cond, "opt", scatter_dimension=1, tiled=True),
        lax.psum_scatter(grad_out, "opt", scatter_dimension=2, tiled=True),
    )
    grad_taps = jnp.stack(tap_grads).reshape(LAYERS, 3, H, 2, H)
    grad_matrices = jnp.transpose(grad_taps, (0, 1, 3, 2, 4)).reshape(NMAT, H, H)
    grad_slots = jnp.take(grad_matrices, soap_slots, axis=0)
    grad_total = lax.psum(grad_slots, ("tm", "opt"))
    grad_owned = lax.dynamic_slice_in_dim(grad_total, lax.axis_index("opt") * owned, owned, 0)
    (
        in_new,
        soap_first_new,
        soap_second_new,
        left_stats_new,
        right_stats_new,
        left_basis_new,
        right_basis_new,
    ) = jax.vmap(soap_update, in_axes=(0, 0, 0, 0, 0, 0, 0, 0, None))(
        in_weight,
        grad_owned,
        soap_first,
        soap_second,
        left_stats,
        right_stats,
        left_basis,
        right_basis,
        steps_done,
    )
    cond_new, cond_first_new, cond_second_new = adamw_update(
        cond_weight, grad_cond, cond_first, cond_second, steps_done, learn_rate
    )
    out_new, out_first_new, out_second_new = adamw_update(
        out_weight, grad_out, out_first, out_second, steps_done, learn_rate
    )
    aux_new, aux_first_new, aux_second_new = adamw_update(
        aux_params, grad_aux, aux_first, aux_second, steps_done, aux_rate
    )
    flow_new, flow_first_new, flow_second_new = adamw_update(
        flow_params, grad_flow, flow_first, flow_second, steps_done, learn_rate
    )
    return (
        loss,
        in_new,
        soap_first_new,
        soap_second_new,
        left_stats_new,
        right_stats_new,
        left_basis_new,
        right_basis_new,
        cond_new,
        cond_first_new,
        cond_second_new,
        out_new,
        out_first_new,
        out_second_new,
        aux_new,
        aux_first_new,
        aux_second_new,
        flow_new,
        flow_first_new,
        flow_second_new,
    )


def solution(mesh):
    placed = (
        P("opt", "tm", None),
        P("opt"),
        P(),
        P("opt", "tm", None),
        P("opt", "tm", None),
        P(),
        P(),
        P("opt", None, None),
        P("opt", None, None),
        P("opt", None, None),
        P("opt", None, None),
        P("opt", None, None),
        P("opt", None, None),
        P("opt", None, None),
        P("tm", "opt"),
        P("tm", "opt"),
        P("tm", "opt"),
        P(None, "tm", "opt"),
        P(None, "tm", "opt"),
        P(None, "tm", "opt"),
        P(),
        P(),
        P(),
        P(),
        P(),
        P(),
    )
    return jax.shard_map(
        shards,
        mesh=mesh,
        in_specs=placed,
        out_specs=(
            P(),
            P("opt", None, None),
            P("opt", None, None),
            P("opt", None, None),
            P("opt", None, None),
            P("opt", None, None),
            P("opt", None, None),
            P("opt", None, None),
            P("tm", "opt"),
            P("tm", "opt"),
            P("tm", "opt"),
            P(None, "tm", "opt"),
            P(None, "tm", "opt"),
            P(None, "tm", "opt"),
            P(),
            P(),
            P(),
            P(),
            P(),
            P(),
        ),
        check_vma=False,
    )
```

profile of v0, /device:TPU:0, one launch (start us, length us, event | category | flops | bytes accessed | tf_op | source)
XLA Modules:
  0.0 1552.6 jit_solution(7028560118544681296)
XLA Ops:
  8.3 8.0 all_gather.15
  39.0 6.1 all_gather.18
  55.9 20.3 %all-gather.4.cloned.1.call-done = bf16[2048,640]{0,1:T(8,128)(2,1)} async-done(((bf16[256,640]{0,1:T(8,128)(2,1)}), bf16[2048,640]{0,1:T(8,128)(2,1)}) %all-gather.4.cloned.1.call-update) | async-done | bytes 2621456 | tf_op jit(solution)/shard_map/all_gather | solution.py:214
  76.2 9.5 fusion.211
  85.7 37.2 %all-gather.6.cloned.1.call-done = bf16[12,512,512]{2,1,0:T(8,128)(2,1)} async-done(((bf16[3,512,512]{2,1,0:T(8,128)(2,1)}), bf16[12,512,512]{2,1,0:T(8,128)(2,1)}) %all-gather.6.cloned.1.call-update) | async-done | bytes 6291472 | tf_op jit(solution)/shard_map/all_gather | solution.py:204
  122.9 7.1 gather_fusion.1
  130.0 12.8 fusion
  191.5 5.5 collective-permute-done.2
  278.4 6.4 maximum_maximum_fusion
  284.8 11.4 gather_fusion.3
  296.2 12.7 copy.448
  308.9 10.9 broadcast_select_fusion.1
  361.0 9.5 collective-permute-done.6
  374.3 6.6 fusion.7
  395.2 47.2 %all-reduce.3 = (f32[2]{0:T(128)S(1)}, f32[17,512]{1,0:T(8,128)S(1)}, f32[6,7]{0,1:T(8,128)S(1)}) all-reduce(f32[2]{0:T(128)S(1)} %copy-done.100, f32[17,512]{1,0:T(8,128)S(1)} %concatenate.110, f32[6,7]{0,1:T(8,128)S(1)} %pad_maximum_fusion.25), channel_id=1, replica_groups=mesh['tm'=8,'opt'=4] {'tm','opt'}, use_global_device_ids=true, to_apply=%region_5.6 | all-reduce | flops 8748 | bytes 69984 | tf_op jit(solution)/shard_map/psum | solution.py:324
  447.4 110.1 %all-reduce.6.cloned.1.call-done = f32[12,512,512]{1,2,0:T(8,128)} async-done(((f32[12,512,512]{1,2,0:T(8,128)}), f32[12,512,512]{1,2,0:T(8,128)}) %all-reduce.6.cloned.1.call-update) | async-done | bytes 12582928 | tf_op jit(solution)/shard_map/psum | solution.py:344
  557.4 8.9 multiply_add_fusion.1
  566.4 5.5 fusion.216
  573.6 7.2 fusion.217
  580.7 8.6 multiply_add_fusion
  596.5 7.6 fusion.220
  613.0 35.2 %custom-call.56 = f32[3,128,128]{2,1,0:T(8,128)S(1)} custom-call(f32[3,128,128]{2,1,0:T(8,128)S(1)} %cholesky.481), custom_call_target="Cholesky" | custom-call | tf_op jit(solution)/shard_map/vmap(jit(cholesky))/cholesky | solution.py:68
  648.2 30.1 %custom-call.57 = f32[3,1,128,128]{2,3,1,0:T(8,128)} custom-call(f32[3,1,128,128]{3,2,1,0:T(8,128)S(1)} %select_bitcast_fusion.2), custom_call_target="InvertDiagBlocksLowerTriangular" | custom-call | tf_op jit(solution)/shard_map/vmap(jit(cholesky))/cholesky | solution.py:68
  685.5 36.0 %custom-call.58 = f32[3,128,128]{2,1,0:T(8,128)} custom-call(f32[3,128,128]{2,1,0:T(8,128)S(1)} %cholesky.485), custom_call_target="Cholesky" | custom-call | tf_op jit(solution)/shard_map/vmap(jit(cholesky))/cholesky | solution.py:68
  731.0 36.0 %custom-call.48 = f32[3,128,128]{2,1,0:T(8,128)S(1)} custom-call(f32[3,128,128]{2,1,0:T(8,128)} %cholesky.468), custom_call_target="Cholesky" | custom-call | tf_op jit(solution)/shard_map/vmap(jit(cholesky))/cholesky | solution.py:68
  768.8 30.9 %custom-call.59 = f32[3,1,128,128]{2,3,1,0:T(8,128)} custom-call(f32[3,1,128,128]{3,2,1,0:T(8,128)} %get-tuple-element.414), custom_call_target="InvertDiagBlocksLowerTriangular" | custom-call | tf_op jit(solution)/shard_map/vmap(jit(cholesky))/cholesky | solution.py:68
  799.7 31.1 %custom-call.49 = f32[3,1,128,128]{2,3,1,0:T(8,128)} custom-call(f32[3,1,128,128]{3,2,1,0:T(8,128)} %get-tuple-element.430), custom_call_target="InvertDiagBlocksLowerTriangular" | custom-call | tf_op jit(solution)/shard_map/vmap(jit(cholesky))/cholesky | solution.py:68
  836.7 36.6 %custom-call.60 = f32[3,128,128]{2,1,0:T(8,128)} custom-call(f32[3,128,128]{2,1,0:T(8,128)} %cholesky.490), custom_call_target="Cholesky" | custom-call | tf_op jit(solution)/shard_map/vmap(jit(cholesky))/cholesky | solution.py:68
  881.2 37.0 %custom-call.50 = f32[3,128,128]{2,1,0:T(8,128)} custom-call(f32[3,128,128]{2,1,0:T(8,128)} %cholesky.472), custom_call_target="Cholesky" | custom-call | tf_op jit(solution)/shard_map/vmap(jit(cholesky))/cholesky | solution.py:68
  920.1 30.9 %custom-call.61 = f32[3,1,128,128]{2,3,1,0:T(8,128)} custom-call(f32[3,1,128,128]{3,2,1,0:T(8,128)} %get-tuple-element.412), custom_call_target="InvertDiagBlocksLowerTriangular" | custom-call | tf_op jit(solution)/shard_map/vmap(jit(cholesky))/cholesky | solution.py:68
  955.9 36.6 %custom-call.62 = f32[3,128,128]{2,1,0:T(8,128)} custom-call(f32[3,128,128]{2,1,0:T(8,128)} %convolution_subtract_fusion.6), custom_call_target="Cholesky" | custom-call | tf_op jit(solution)/shard_map/vmap(jit(cholesky))/cholesky | solution.py:68
  992.6 31.1 %custom-call.51 = f32[3,1,128,128]{2,3,1,0:T(8,128)} custom-call(f32[3,1,128,128]{3,2,1,0:T(8,128)} %get-tuple-element.429), custom_call_target="InvertDiagBlocksLowerTriangular" | custom-call | tf_op jit(solution)/shard_map/vmap(jit(cholesky))/cholesky | solution.py:68
  1029.6 36.6 %custom-call.52 = f32[3,128,128]{2,1,0:T(8,128)} custom-call(f32[3,128,128]{2,1,0:T(8,128)} %cholesky.477), custom_call_target="Cholesky" | custom-call | tf_op jit(solution)/shard_map/vmap(jit(cholesky))/cholesky | solution.py:68
  1067.9 30.9 %custom-call.53 = f32[3,1,128,128]{2,3,1,0:T(8,128)} custom-call(f32[3,1,128,128]{3,2,1,0:T(8,128)} %get-tuple-element.416), custom_call_target="InvertDiagBlocksLowerTriangular" | custom-call | tf_op jit(solution)/shard_map/vmap(jit(cholesky))/cholesky | solution.py:68
  1103.7 36.8 %custom-call.54 = f32[3,128,128]{2,1,0:T(8,128)} custom-call(f32[3,128,128]{2,1,0:T(8,128)} %convolution_subtract_fusion.7), custom_call_target="Cholesky" | custom-call | tf_op jit(solution)/shard_map/vmap(jit(cholesky))/cholesky | solution.py:68
  1143.4 7.1 select_select_fusion
  1151.5 14.8 while.18
  1166.2 119.3 %custom-call.63 = f32[3,4,128,128]{2,3,1,0:T(8,128)} custom-call(f32[3,4,128,128]{3,2,1,0:T(8,128)} %bitcast.409), custom_call_target="InvertDiagBlocksLowerTriangular" | custom-call | tf_op jit(solution)/shard_map/vmap(jit(_solve_triangular))/triangular_solve | solution.py:69
  1286.5 14.8 while.17
  1301.3 119.7 %custom-call.55 = f32[3,4,128,128]{2,3,1,0:T(8,128)} custom-call(f32[3,4,128,128]{3,2,1,0:T(8,128)} %bitcast.408), custom_call_target="InvertDiagBlocksLowerTriangular" | custom-call | tf_op jit(solution)/shard_map/vmap(jit(_solve_triangular))/triangular_solve | solution.py:69
  1463.2 7.7 fusion.28
  1470.9 7.2 fusion.15
  1478.2 6.0 fusion.81
  1484.2 5.5 fusion.218
  1489.7 7.1 fusion.51
  1496.9 14.3 fusion.18
  1520.8 9.8 fusion.49
  1530.7 7.1 multiply_subtract_fusion
  (493 shorter events, 388.3 us)
Async XLA Ops:
  7.2 582.2 %copy-start = (f32[3,512,512]{2,1,0:T(8,128)S(1)}, f32[3,512,512]{2,1,0:T(8,128)}, u32[]{:S(2)}) copy-start(f32[3,512,512]{2,1,0:T(8,128)} %param.64) | copy-start | bytes 9437188
  7.2 69.0 %all-gather.4.cloned.1.call-start = ((), (), s32[]{:S(2)}) async-start(), calls=%async_computation.4 | async-start | bytes 2949120 | tf_op jit(solution)/shard_map/all_gather | solution.py:214
  16.4 10.3 copy-start.102
  16.4 106.5 %all-gather.6.cloned.1.call-start = ((), (), s32[]{:S(2)}) async-start(), calls=%async_computation.5 | async-start | bytes 7864320 | tf_op jit(solution)/shard_map/all_gather | solution.py:204
  19.7 7.7 copy-start.89
  19.7 7.8 copy-start.92
  19.7 158.6 %all-gather.8.cloned.1.call-start = ((), (), s32[]{:S(2)}) async-start(), calls=%async_computation.6 | async-start | bytes 1769472 | tf_op jit(solution)/shard_map/all_gather | solution.py:215
  24.3 14.7 copy-start.87
  25.5 19.7 %copy-start.103 = (s32[12]{0:T(128)S(1)}, s32[12]{0:T(128)}, u32[]{:S(2)}) copy-start(s32[12]{0:T(128)} %param.56) | copy-start | bytes 148
  25.5 21.0 %copy-start.97 = (bf16[2,16,80]{2,1,0:T(8,128)(2,1)S(1)}, bf16[2,16,80]{2,1,0:T(8,128)(2,1)}, u32[]{:S(2)}) copy-start(bf16[2,16,80]{2,1,0:T(8,128)(2,1)} %param.54) | copy-start | bytes 15364
  32.5 20.9 %collective-permute-start.1 = (bf16[2,64,512]{2,1,0:T(8,128)(2,1)}, bf16[2,64,512]{2,1,0:T(8,128)(2,1)}, u32[]{:S(2)}, u32[]{:S(2)}) collective-permute-start(bf16[2,64,512]{2,1,0:T(8,128)(2,1)} %get-tuple-element.406), channel_id=1, source_target_pairs={{4,0},{8,4},{12,8},{16,12},{20,16},{24,20},{28,24},{5,1},{9,5},{13... | collective-permute-start | bytes 393224 | tf_op jit(solution)/shard_map/ppermute | solution.py:36
  33.8 19.6 %collective-permute-start = (bf16[2,64,512]{2,1,0:T(8,128)(2,1)S(1)}, bf16[2,64,512]{2,1,0:T(8,128)(2,1)}, u32[]{:S(2)}, u32[]{:S(2)}) collective-permute-start(bf16[2,64,512]{2,1,0:T(8,128)(2,1)S(1)} %get-tuple-element.407), channel_id=1, source_target_pairs={{0,4},{4,8},{8,12},{12,16},{16,20},{20,24},{24,28},{1,5},{5,9},{9,... | collective-permute-start | bytes 393224 | tf_op jit(solution)/shard_map/ppermute | solution.py:34
  45.1 512.3 %all-reduce.6.cloned.1.call-start = ((), (), s32[]{:S(2)}) async-start(), calls=%async_computation.7 | async-start | bytes 25165824 | tf_op jit(solution)/shard_map/psum | solution.py:344
  178.3 9.2 copy-start.78
  181.2 10.3 collective-permute-start.3
  182.5 14.5 collective-permute-start.2
  189.2 8.0 copy-start.77
  189.2 9.3 slice-start.2
  210.0 15.8 %copy-start.28 = (bf16[1024,512]{1,0:T(8,128)(2,1)}, bf16[1024,512]{1,0:T(8,128)(2,1)S(1)}, u32[]{:S(2)}) copy-start(bf16[1024,512]{1,0:T(8,128)(2,1)S(1)} %get-tuple-element.388) | copy-start | bytes 3145732
  210.0 15.8 %copy-start.30 = (bf16[1024,512]{1,0:T(8,128)(2,1)}, bf16[1024,512]{1,0:T(8,128)(2,1)S(1)}, u32[]{:S(2)}) copy-start(bf16[1024,512]{1,0:T(8,128)(2,1)S(1)} %get-tuple-element.389) | copy-start | bytes 3145732
  219.1 16.8 %collective-permute-start.4 = (f32[2,128,512]{2,1,0:T(8,128)}, f32[2,128,512]{2,1,0:T(8,128)}, u32[]{:S(2)}, u32[]{:S(2)}) collective-permute-start(f32[2,128,512]{2,1,0:T(8,128)} %slice.656), channel_id=1, source_target_pairs={{0,4},{4,8},{8,12},{12,16},{16,20},{20,24},{24,28},{1,5},{5,9},{9,... | collective-permute-start | bytes 1572872 | tf_op jit(solution)/shard_map/ppermute | solution.py:34
  231.3 8.4 copy-start.53
  238.4 15.8 %collective-permute-start.5 = (f32[2,128,512]{2,1,0:T(8,128)}, f32[2,128,512]{2,1,0:T(8,128)}, u32[]{:S(2)}, u32[]{:S(2)}) collective-permute-start(f32[2,128,512]{2,1,0:T(8,128)} %get-tuple-element.396), channel_id=1, source_target_pairs={{4,0},{8,4},{12,8},{16,12},{20,16},{24,20},{28,24},{5,1},{9,5},{13... | collective-permute-start | bytes 1572872 | tf_op jit(solution)/shard_map/ppermute | solution.py:36
  245.7 12.4 copy-start.66
  250.3 7.8 copy-start.18
  319.8 1177.1 %reduce-scatter.9.cloned.1.call-start = ((), (), s32[]{:S(2)}) async-start(), calls=%async_computation.9 | async-start | bytes 3538944 | tf_op jit(solution)/shard_map/reduce_scatter | solution.py:335
  327.2 1184.0 %reduce-scatter.7.cloned.1.call-start = ((), (), s32[]{:S(2)}) async-start(), calls=%async_computation.8 | async-start | bytes 5898240 | tf_op jit(solution)/shard_map/reduce_scatter | solution.py:334
  355.7 14.8 collective-permute-start.6
  360.8 13.5 copy-start.29
  360.8 13.5 copy-start.31
  360.8 13.5 copy-start.70
  372.6 11.3 collective-permute-start.7
  394.6 52.1 %copy-start.94 = (f32[17,512]{1,0:T(8,128)S(1)}, f32[17,512]{1,0:T(8,128)}, u32[]{:S(2)}) copy-start(f32[17,512]{1,0:T(8,128)} %param.73) | copy-start | bytes 104452
  394.6 52.1 %copy-start.95 = (f32[17,512]{1,0:T(8,128)S(1)}, f32[17,512]{1,0:T(8,128)}, u32[]{:S(2)}) copy-start(f32[17,512]{1,0:T(8,128)} %param.72) | copy-start | bytes 104452
  394.8 1142.9 %reduce-scatter.11.cloned.1.call-start = ((), (), s32[]{:S(2)}) async-start(), calls=%async_computation.10 | async-start | bytes 491520 | tf_op jit(solution)/shard_map/reduce_scatter | solution.py:339
  557.4 8.9 copy-start.8
  1423.3 15.1 copy-start.6
  1427.2 11.2 copy-start.12
  1447.2 8.7 copy-start.5
  1451.1 10.3 copy-start.11
  1456.0 7.2 copy-start.19
  1456.0 7.2 copy-start.9
  1463.2 7.7 copy-start.61
  1470.9 7.2 copy-start.59
  1496.9 45.6 %reduce-scatter.13.cloned.1.call-start = ((), (), s32[]{:S(2)}) async-start(), calls=%async_computation.11 | async-start | bytes 819200
  1520.8 9.8 copy-start.22
  1520.8 9.8 copy-start.60
  1530.6 11.8 copy-start.86
  (77 other events, 246.7 us)
Sparse Core Ops, SparseCore 0:
  16.5 59.6 all-gather.3
  78.4 44.5 all-gather.5
  125.1 44.1 all-gather.7
  319.9 237.5 all-reduce.5
  560.9 74.4 reduce-scatter.8
  638.9 102.1 reduce-scatter.6
  1497.0 20.4 reduce-scatter.10
  1520.0 22.4 reduce-scatter.12
where the time goes:
time: 1560 us; the launch traced here: 1550 us
  other arithmetic  817 us (52%)
  matrix products  257 us (16%)
  waiting for transfers between devices  192 us (12%)
  local copies, waits for them, and re-layouts  177 us (11%)
  blocking collectives  61.3 us (4%)
  starting transfers between devices  25.4 us (2%)
  between operations  22.7 us (1%)
    another operation x27, other arithmetic, orthonormal(): factor = jnp.linalg.cholesky(full_dot(matrix.T, matrix))  485 us
    another operation x5, other arithmetic, orthonormal(): return jax.scipy.linalg.solve_triangular(factor, matrix.T, lower=True).T  248 us
    dot_general x20, matrix products, full_dot(): jnp.dot(matrix_a, matrix_b, precision=highest, preferred_element_type=jnp...  119 us
    psum x1, waiting for transfers between devices, shards(): grad_total = lax.psum(grad_slots, ('tm', 'opt'))  110 us
    unnamed x241, local copies, waits for them, and re-layouts  50 us
    psum x1, blocking collectives, shards(): lax.psum((jnp.stack([final_part, early_part]), grad_aux, grad_flow), ('tm...  47.2 us
    all_gather x1, waiting for transfers between devices, shards(): lax.all_gather(in_weight.astype(jnp.bfloat16), 'opt', axis=0, tiled=True)  37.2 us
    another operation x14, matrix products, orthonormal(): return jax.scipy.linalg.solve_triangular(factor, matrix.T, lower=True).T  35.3 us
  transfers between devices with their start and end apart: 16, of which 9 were waited for; matrix products, arithmetic and copies ran while one was open for 73% of the time, Pallas kernels for 0%

commit v1 on v0

--- a/solution.py
+++ b/solution.py
@@ -1,6 +1,8 @@
 import jax
 import jax.numpy as jnp
 from jax import lax
+from jax.experimental import pallas as pl
+from jax.experimental.pallas import tpu as pltpu
 from jax.sharding import PartitionSpec as P
 
 H = 512
@@ -64,9 +66,183 @@
     )
 
 
-def orthonormal(matrix):
-    factor = jnp.linalg.cholesky(full_dot(matrix.T, matrix))
-    return jax.scipy.linalg.solve_triangular(factor, matrix.T, lower=True).T
+def _nt(x, y, precision=highest):
+    return lax.dot_general(x, y, (((1,), (1,)), ((), ())), precision=precision, preferred_element_type=jnp.float32)
+
+def _nn(x, y, precision=highest):
+    return lax.dot_general(x, y, (((1,), (0,)), ((), ())), precision=precision, preferred_element_type=jnp.float32)
+
+def _split(x):
+    hi = x.astype(jnp.bfloat16)
+    return hi, (x - hi.astype(jnp.float32)).astype(jnp.bfloat16)
+
+def _three(dims, x, y):
+    xh, xl = x
+    yh, yl = y
+    dot = lambda a, b: lax.dot_general(a, b, dims, preferred_element_type=jnp.float32)
+    return dot(xh, yh) + (dot(xh, yl) + dot(xl, yh))
+
+NT = (((1,), (1,)), ((), ()))
+NN = (((1,), (0,)), ((), ()))
+
+def pair_inverse(blocks):
+    lane = lax.broadcasted_iota(jnp.int32, (8, 128), 1)
+    sub = lax.broadcasted_iota(jnp.int32, (8, 128), 0)
+    local = lane % 64
+    half = lane - local
+    groups = [[block[8 * g:8 * g + 8] for g in range(8)] for block in blocks]
+    for start in range(0, 64, 4):
+        first, low = divmod(start, 8)
+        inside = (local >= start) & (local < start + 4)
+        for rows in groups:
+            cols = []
+            for n in range(4):
+                pick = half + (start + n)
+                cols.append([jnp.take_along_axis(rows[g], pick, axis=1, mode="promise_in_bounds") for g in range(first, 8)])
+            lead = rows[first]
+            entry = [[cols[n][0][low + m:low + m + 1] for n in range(m + 1)] for m in range(4)]
+            work = [jnp.where(local == start + m, 1.0, jnp.where(inside, 0.0, jnp.broadcast_to(lead[low + m:low + m + 1], (8, 128)))) for m in range(4)]
+            entry = [[jnp.broadcast_to(e, (8, 128)) for e in line] for line in entry]
+            scaled = []
+            ratio = {}
+            for m in range(4):
+                inverse = 1.0 / entry[m][m]
+                for n in range(m + 1, 4):
+                    ratio[n, m] = entry[n][m] * inverse
+                for n in range(m + 1, 4):
+                    work[n] = work[n] - ratio[n, m] * work[m]
+                    for q in range(m + 1, n + 1):
+                        entry[n][q] = entry[n][q] - ratio[n, m] * entry[q][m]
+                scaled.append(work[m] * inverse)
+            final = [work[m] * lax.rsqrt(entry[m][m]) for m in range(4)]
+            for m in (2, 1, 0):
+                for n in range(m + 1, 4):
+                    scaled[m] = scaled[m] - ratio[n, m] * scaled[n]
+            for g in range(first, 8):
+                old = jnp.where(inside, 0.0, rows[g])
+                new = old
+                for n in range(4):
+                    new = new - cols[n][g - first] * scaled[n]
+                if g == first:
+                    kept = rows[g]
+                    for m in range(4):
+                        kept = jnp.where(sub == low + m, final[m], kept)
+                    new = jnp.where(sub >= low + 4, new, kept)
+                rows[g] = new
+    return [
+        jnp.concatenate([jnp.where(local <= 8 * g + sub, rows[g], 0.0) for g in range(8)], axis=0)
+        for rows in groups
+    ]
+
+def beside(x, y):
+    return jnp.concatenate([x, y], axis=1)
+
+def paired(block):
+    wide = jnp.concatenate([block, block], axis=0)
+    row = lax.broadcasted_iota(jnp.int32, (128, 128), 0)
+    col = lax.broadcasted_iota(jnp.int32, (128, 128), 1)
+    return jnp.where((row // 64) == (col // 64), wide, 0.0)
+
+def factor_kernel(gram_ref, tall_ref, out_ref, s_ref, a_ref, y_ref, l_ref, w_ref):
+    count = gram_ref.shape[0]
+    step = pl.program_id(0)
+
+    @pl.when(step == 0)
+    def _():
+        s_ref[...] = gram_ref[...]
+        a_ref[...] = tall_ref[...]
+
+    start = pl.multiple_of(step * 128, 128)
+    diag = [s_ref[i, pl.ds(start, 128), pl.ds(start, 128)] for i in range(count)]
+    pairs = range(count // 2)
+    top = pair_inverse([beside(diag[2 * p][:64, :64], diag[2 * p + 1][:64, :64]) for p in pairs])
+    cross, below = [], []
+    for p in pairs:
+        low = beside(diag[2 * p][64:, :64], diag[2 * p + 1][64:, :64])
+        factor = _nt(low, paired(top[p]))
+        cross.append(factor)
+        rest = beside(diag[2 * p][64:, 64:], diag[2 * p + 1][64:, 64:])
+        below.append(rest - _nt(factor, paired(factor)))
+    bottom = pair_inverse(below)
+    for p in pairs:
+        corner = -_nn(_nn(bottom[p], paired(cross[p])), paired(top[p]))
+        zero = jnp.zeros((64, 64), jnp.float32)
+        for side in range(2):
+            cut = slice(64 * side, 64 * side + 64)
+            w_ref[2 * p + side, :64] = beside(top[p][:, cut], zero)
+            w_ref[2 * p + side, 64:] = beside(corner[:, cut], bottom[p][:, cut])
+
+    @pl.when(step % 2 == 0)
+    def _():
+        for i in range(count):
+            inv = w_ref[i]
+            y_ref[i, :128, :128] = inv
+            y_ref[i, :128, 128:] = jnp.zeros((128, 128), jnp.float32)
+            low = s_ref[i, pl.ds(start + 128, 128), pl.ds(start, 128)]
+            factor = _nt(low, inv)
+            l_ref[i] = factor
+            s_ref[i, pl.ds(start + 128, 128), pl.ds(start + 128, 128)] -= _nt(factor, factor)
+
+    @pl.when(step % 2 == 1)
+    def _():
+        for i in range(count):
+            inv = w_ref[i]
+            y_ref[i, 128:, :128] = -_nn(_nn(inv, l_ref[i]), y_ref[i, :128, :128])
+            y_ref[i, 128:, 128:] = inv
+
+    @pl.when(step == 1)
+    def _():
+        for i in range(count):
+            inv = y_ref[i]
+            factor = _nt(s_ref[i, 256:, :256], inv)
+            s_ref[i, 256:, 256:] -= _nt(factor, factor)
+            inv = _split(inv)
+            done = _three(NT, _split(a_ref[i, :, :256]), inv)
+            out_ref[i, :, :256] = done
+            a_ref[i, :, 256:] -= _three(NT, _split(done), _split(factor))
+
+    @pl.when(step == 3)
+    def _():
+        for i in range(count):
+            out_ref[i, :, 256:] = _three(NT, _split(a_ref[i, :, 256:]), _split(y_ref[i]))
+
+def orthonormal_all(gram, tall):
+    count = gram.shape[0]
+    whole = lambda: pl.BlockSpec(memory_space=pltpu.VMEM)
+    return pl.pallas_call(
+        factor_kernel,
+        grid=(4,),
+        out_shape=jax.ShapeDtypeStruct(tall.shape, jnp.float32),
+        in_specs=[whole(), whole()],
+        out_specs=whole(),
+        scratch_shapes=[
+            pltpu.VMEM((count, 512, 512), jnp.float32),
+            pltpu.VMEM((count, 512, 512), jnp.float32),
+            pltpu.VMEM((count, 256, 256), jnp.float32),
+            pltpu.VMEM((count, 128, 128), jnp.float32),
+            pltpu.VMEM((count, 128, 128), jnp.float32),
+        ],
+    )(gram, tall)
+
+
+def high_dot(matrix_a, matrix_b, dims):
+    return lax.dot_general(
+        matrix_a, matrix_b, dims, precision=lax.Precision.HIGH, preferred_element_type=jnp.float32
+    )
+
+
+def low_dot(matrix_a, matrix_b, dims):
+    return lax.dot_general(
+        matrix_a.astype(jnp.bfloat16),
+        matrix_b.astype(jnp.bfloat16),
+        dims,
+        preferred_element_type=jnp.float32,
+    )
+
+
+PLAIN = (((2,), (1,)), ((0,), (0,)))
+FIRST = (((1,), (1,)), ((0,), (0,)))
+SECOND = (((2,), (2,)), ((0,), (0,)))
 
 
 def soap_update(
@@ -80,7 +256,9 @@
     right_basis,
     steps_done,
 ):
-    rotated = full_dot(full_dot(left_basis.T, gradient), right_basis)
+    owned = weight.shape[0]
+    turned = high_dot(left_basis, gradient.astype(jnp.float32), FIRST)
+    rotated = high_dot(turned, right_basis, PLAIN)
     moment_one = beta_first * moment_one + (1.0 - beta_first) * rotated
     moment_two = beta_second * moment_two + (1.0 - beta_second) * rotated * rotated
     direction = (
@@ -89,15 +267,83 @@
         / (jnp.sqrt(moment_two / (1.0 - beta_second**steps_done)) + epsilon)
     )
     weight = weight - learn_rate * (
-        full_dot(full_dot(left_basis, direction), right_basis.T) + decay_weight * weight
-    )
-    left_stats = beta_stats * left_stats + (1.0 - beta_stats) * full_dot(gradient, gradient.T)
-    right_stats = beta_stats * right_stats + (1.0 - beta_stats) * full_dot(gradient.T, gradient)
-    left_new = orthonormal(full_dot(left_stats, left_basis))
-    right_new = orthonormal(full_dot(right_stats, right_basis))
-    initial = full_dot(full_dot(left_basis, moment_one), right_basis.T)
-    moment_one = full_dot(full_dot(left_new.T, initial), right_new)
+        low_dot(low_dot(left_basis, direction, PLAIN), right_basis, SECOND) + decay_weight * weight
+    )
+    left_stats = beta_stats * left_stats + (1.0 - beta_stats) * low_dot(gradient, gradient, SECOND)
+    right_stats = beta_stats * right_stats + (1.0 - beta_stats) * low_dot(gradient, gradient, FIRST)
+    tall = jnp.concatenate(
+        [high_dot(left_stats, left_basis, PLAIN), high_dot(right_stats, right_basis, PLAIN)], axis=0
+    )
+    bases = orthonormal_all(high_dot(tall, tall, FIRST), tall)
+    left_new, right_new = bases[:owned], bases[owned:]
+    initial = high_dot(high_dot(left_basis, moment_one, PLAIN), right_basis, SECOND)
+    moment_one = high_dot(high_dot(left_new, initial, FIRST), right_new, PLAIN)
     return (weight, moment_one, moment_two, left_stats, right_stats, left_new, right_new)
+
+
+def swap(values, axis, bit):
+    return lax.ppermute(values, axis, [(i, i ^ bit) for i in range(lax.axis_size(axis))])
+
+
+def side_of(axis, bit):
+    return (lax.axis_index(axis) // bit) % 2
+
+
+def ordered(values, others, axis, bit, dim):
+    first = side_of(axis, bit) == 0
+    return jnp.concatenate(
+        [jnp.where(first, values, others), jnp.where(first, others, values)], axis=dim
+    )
+
+
+def halves(values, axis, bit, dim):
+    width = values.shape[dim] // 2
+    side = side_of(axis, bit)
+    return (
+        lax.dynamic_slice_in_dim(values, side * width, width, dim),
+        lax.dynamic_slice_in_dim(values, (1 - side) * width, width, dim),
+    )
+
+
+def bits_of(axis):
+    count = lax.axis_size(axis)
+    return [1 << i for i in range(count.bit_length() - 1)]
+
+
+def scatter_half(values, axis, bit, dim):
+    kept, sent = halves(values, axis, bit, dim)
+    return kept + swap(sent, axis, bit)
+
+
+def all_sum(values):
+    for axis in ("opt", "tm"):
+        for bit in bits_of(axis):
+            values = values + swap(values, axis, bit)
+    return values
+
+
+def gather_blocks(values, axis, bits):
+    for bit in bits:
+        values = ordered(values, swap(values, axis, bit), axis, bit, 0)
+    return values
+
+
+def reduce_slots(own_core, owned):
+    pieces = []
+    low = own_core.astype(jnp.bfloat16)
+    kept, sent = halves(low, "opt", 1, 1)
+    low = (kept + swap(sent, "opt", 1))[:, 0]
+    kept, sent = halves(low, "opt", 2, 0)
+    for slot in range(owned):
+        part = kept[0, slot] + swap(sent[0, slot], "opt", 2)
+        bits = bits_of("tm")
+        for bit in bits[:-1]:
+            part = scatter_half(part, "tm", bit, 0)
+        part = part + swap(part, "tm", bits[-1])
+        for bit in reversed(bits[:-1]):
+            part = ordered(part, swap(part, "tm", bit), "tm", bit, 0)
+        pieces.append(part)
+    return jnp.stack(pieces)
 
 
 def adamw_update(weight, gradient, moment_one, moment_two, steps_done, rate_value):
@@ -201,19 +447,32 @@
     scale_early = early_weight / (2.0 * tokens_all)
     steps_done = step_count[0].astype(jnp.float32)
     owned = NMAT // lax.axis_size("opt")
-    slot_weights = lax.all_gather(in_weight.astype(jnp.bfloat16), "opt", axis=0, tiled=True)
+    opt_bits, tm_bits = bits_of("opt"), bits_of("tm")
+    own = in_weight.astype(jnp.bfloat16)
+    across = swap(own, "opt", 2)
+    own_x = ordered(own[None], swap(own, "opt", 1)[None], "opt", 1, 0)
+    other_x = ordered(across[None], swap(across, "opt", 1)[None], "opt", 1, 0)
+    slot_weights = ordered(own_x, other_x, "opt", 2, 0).reshape(NMAT, H, H)
     matrices = jnp.take(slot_weights, jnp.argsort(soap_slots), axis=0)
     every_tap_weight = jnp.transpose(matrices.reshape(LAYERS, 3, 2, H, H), (0, 1, 3, 2, 4)).reshape(
         LAYERS, 3, H, 2 * H
     )
-    cond_cols, out_cols = (
-        lax.all_gather(cond_weight.astype(jnp.bfloat16), "opt", axis=1, tiled=True),
-        lax.all_gather(out_weight.astype(jnp.bfloat16), "opt", axis=2, tiled=True),
-    )
-    cond_full, out_full = (
-        lax.all_gather(cond_cols, "tm", axis=0, tiled=True),
-        lax.all_gather(out_cols, "tm", axis=1, tiled=True),
-    )
+    cond_part = cond_weight.astype(jnp.bfloat16)
+    cond_part = ordered(cond_part, swap(cond_part, "opt", 2), "opt", 2, 1)
+    cond_part = gather_blocks(cond_part, "tm", tm_bits)
+    cond_other = swap(cond_part, "opt", 1)
+    cond_rows = cond_part.shape[0]
+    cond_full = ordered(
+        cond_part.reshape(cond_rows, 2, 1, -1), cond_other.reshape(cond_rows, 2, 1, -1), "opt", 1, 2
+    ).reshape(cond_rows, -1)
+    out_part = jnp.swapaxes(out_weight.astype(jnp.bfloat16), 0, 1)
+    out_part = ordered(out_part, swap(out_part, "opt", 2), "opt", 2, 2)
+    out_part = gather_blocks(out_part, "tm", tm_bits)
+    out_other = swap(out_part, "opt", 1)
+    out_full = ordered(
+        out_part.reshape(H, 3, 2, 1, -1), out_other.reshape(H, 3, 2, 1, -1), "opt", 1, 3
+    ).reshape(H, 3, H)
+    out_full = jnp.swapaxes(out_full, 0, 1)
 
     def squeeze_one(samples, offset):
         segment = lax.dynamic_slice_in_dim(samples, offset, 8 * G_DEV, 0)
@@ -321,28 +580,37 @@
         ],
         axis=0,
     )
-    parts, grad_aux, grad_flow = lax.psum(
-        (jnp.stack([final_part, early_part]), grad_aux, grad_flow), ("tm", "opt")
-    )
+    small = jnp.concatenate(
+        [grad_aux.reshape(-1), grad_flow.reshape(-1), jnp.stack([final_part, early_part])]
+    )
+    filled = small.shape[0]
+    small = jnp.pad(small, (0, -filled % 1024)).reshape(-1, 128)
+    small = all_sum(small).reshape(-1)
+    grad_aux = small[: grad_aux.size].reshape(grad_aux.shape)
+    grad_flow = small[grad_aux.size : filled - 2].reshape(grad_flow.shape)
+    parts = small[filled - 2 : filled]
     factor = jnp.linalg.cholesky(full_dot(flow_matrix, flow_matrix.T))
     log_det = jnp.sum(jnp.log(jnp.diagonal(factor)))
     inverse_t = jax.scipy.linalg.cho_solve((factor, True), flow_matrix)
     grad_flow = grad_flow.at[:, :6].add(-inverse_t / 6.0)
     loss = parts[0] * scale_final + parts[1] * scale_early - log_det / 6.0
     grad_cond = rows_dot(jnp.concatenate(spectral_grads, axis=1), conditioning)
-    grad_cond, grad_out = (
-        lax.psum_scatter(grad_cond, "tm", scatter_dimension=0, tiled=True),
-        lax.psum_scatter(jnp.stack(out_grads), "tm", scatter_dimension=1, tiled=True),
-    )
-    grad_cond, grad_out = (
-        lax.psum_scatter(grad_cond, "opt", scatter_dimension=1, tiled=True),
-        lax.psum_scatter(grad_out, "opt", scatter_dimension=2, tiled=True),
-    )
+    grad_cond = grad_cond.astype(jnp.bfloat16).reshape(4 * H, 2, 2, -1)
+    grad_out = jnp.stack(out_grads).astype(jnp.bfloat16).reshape(3, H, 2, 2, -1)
+    grad_cond = scatter_half(grad_cond, "opt", 1, 2)
+    grad_out = scatter_half(grad_out, "opt", 1, 3)
+    grad_cond = scatter_half(grad_cond, "opt", 2, 1)
+    grad_out = scatter_half(grad_out, "opt", 2, 2)
+    grad_cond = grad_cond.reshape(4 * H, -1)
+    grad_out = grad_out.reshape(3, H, -1)
+    for bit in reversed(tm_bits):
+        grad_cond = scatter_half(grad_cond, "tm", bit, 0)
+        grad_out = scatter_half(grad_out, "tm", bit, 1)
+    grad_cond, grad_out = grad_cond.astype(jnp.float32), grad_out.astype(jnp.float32)
     grad_taps = jnp.stack(tap_grads).reshape(LAYERS, 3, H, 2, H)
     grad_matrices = jnp.transpose(grad_taps, (0, 1, 3, 2, 4)).reshape(NMAT, H, H)
     grad_slots = jnp.take(grad_matrices, soap_slots, axis=0)
-    grad_total = lax.psum(grad_slots, ("tm", "opt"))
-    grad_owned = lax.dynamic_slice_in_dim(grad_total, lax.axis_index("opt") * owned, owned, 0)
+    grad_owned = reduce_slots(grad_slots.reshape(2, 2, owned, H, H), owned)
     (
         in_new,
         soap_first_new,
@@ -351,7 +619,7 @@
         right_stats_new,
         left_basis_new,
         right_basis_new,
-    ) = jax.vmap(soap_update, in_axes=(0, 0, 0, 0, 0, 0, 0, 0, None))(
+    ) = soap_update(
         in_weight,
         grad_owned,
         soap_first,

time: 1560 us -> 646 us (0.41)
  other arithmetic: 817 us -> 73.4 us
  matrix products: 257 us -> 141 us
  local copies, waits for them, and re-layouts: 177 us -> 111 us
  blocking collectives: 61.3 us -> 0 us
  Pallas kernels: 0 us -> 59.8 us
  starting transfers between devices: 25.4 us -> 69.4 us
  waiting for transfers between devices: 192 us -> 173 us
    another operation x34 -> x4, other arithmetic: 735 us -> 0.28 us  [the longest x1 0.17 us: shards(): grad_out = jnp.stack(out_grads).astype(jnp.bfloat16).reshape(3, H, 2, 2, -1)]
    ppermute x0 -> x47, waiting for transfers between devices: none -> 165 us  [swap(): lax.ppermute(values, axis, [(i, i ^ bit) for i in range(lax.axis_size(axi...]
    psum x1 -> x0, waiting for transfers between devices: 110 us -> none  [shards(): grad_total = lax.psum(grad_slots, ('tm', 'opt'))]
    dot_general x20 -> x6, matrix products: 119 us -> 9.11 us  [full_dot(): jnp.dot(matrix_a, matrix_b, precision=highest, preferred_element_type=jnp...]
    another operation x26 -> x0, matrix products: 62.5 us -> none  [the longest x14 35.3 us: orthonormal(): return jax.scipy.linalg.solve_triangular(factor, matrix.T, lower=True).T]
    pallas_call x0 -> x1, Pallas kernels: none -> 59.8 us  [orthonormal_all(): pl.pallas_call(factor_kernel, grid=(4,), out_shape=jax.ShapeDtypeStruct(t...]
    dot_general x0 -> x12, matrix products: none -> 58.9 us  [the longest x9 46.5 us: high_dot(): lax.dot_general(matrix_a, matrix_b, dims, precision=lax.Precision.HIGH, p...]
    all_gather x3 -> x0, waiting for transfers between devices: 57.5 us -> none  [the longest x1 37.2 us: shards(): lax.all_gather(in_weight.astype(jnp.bfloat16), 'opt', axis=0, tiled=True)]
  transfers between devices with their start and end apart: 16 -> 55, of which waited for: 9 -> 34; matrix products, arithmetic and copies ran while one was open for 73% -> 24% of each run, Pallas kernels for 0% -> 0%
where the time goes in v1:
time: 646 us; the launch traced here: 637 us
  waiting for transfers between devices  173 us (27%)
  matrix products  141 us (22%)
  local copies, waits for them, and re-layouts  111 us (17%)
  other arithmetic  73.4 us (11%)
  starting transfers between devices  69.4 us (11%)
  Pallas kernels  59.8 us (9%)
  between operations  9.56 us (1%)
    ppermute x47, waiting for transfers between devices, swap(): lax.ppermute(values, axis, [(i, i ^ bit) for i in range(lax.axis_size(axi...  165 us
    pallas_call x1, Pallas kernels, orthonormal_all(): pl.pallas_call(factor_kernel, grid=(4,), out_shape=jax.ShapeDtypeStruct(t...  59.8 us
    dot_general x9, matrix products, high_dot(): lax.dot_general(matrix_a, matrix_b, dims, precision=lax.Precision.HIGH, p...  46.5 us
    ppermute x47, starting transfers between devices, swap(): lax.ppermute(values, axis, [(i, i ^ bit) for i in range(lax.axis_size(axi...  44.1 us
    dot_general x13, matrix products, rows_dot(): lax.dot_general(matrix_a, matrix_b, (((0,), (0,)), ((), ())), precision=e...  33.8 us
    unnamed x254, local copies, waits for them, and re-layouts  25.5 us
    dot_general x10, matrix products, cols_dot(): lax.dot_general(matrix_a, matrix_b, (((1,), (1,)), ((), ())), preferred_e...  20.4 us
    ppermute x4, starting transfers between devices, with_halo(): lax.ppermute(tail, axis, [(i, (i + 1) % count) for i in range(ends)])  20 us
  transfers between devices with their start and end apart: 55, of which 34 were waited for; matrix products, arithmetic and copies ran while one was open for 24% of the time, Pallas kernels for 0%

profile of v1, /device:TPU:0, one launch (start us, length us, event | category | flops | bytes accessed | tf_op | source)
XLA Modules:
  0.0 637.0 jit_solution(563153113711677739)
XLA Ops:
  9.4 4.4 while.12
  19.7 4.1 collective-permute-start.5
  31.4 12.2 %collective-permute-done.10 = bf16[64,3,128]{2,0,1:T(8,128)(2,1)S(1)} collective-permute-done((bf16[64,3,128]{2,0,1:T(8,128)(2,1)S(1)}, bf16[64,3,128]{2,0,1:T(8,128)(2,1)S(1)}, u32[]{:S(2)}, u32[]{:S(2)}) %collective-permute-start.10) | collective-permute-done | bytes 49184 | tf_op jit(solution)/shard_map/ppermute | solution.py:285
  52.7 8.6 %collective-permute-done.12 = bf16[128,3,256]{2,0,1:T(8,128)(2,1)S(1)} collective-permute-done((bf16[128,3,256]{2,0,1:T(8,128)(2,1)S(1)}, bf16[128,3,256]{2,0,1:T(8,128)(2,1)S(1)}, u32[]{:S(2)}, u32[]{:S(2)}) %collective-permute-start.12) | collective-permute-done | bytes 196640 | tf_op jit(solution)/shard_map/ppermute | solution.py:285
  69.5 24.1 %collective-permute-done.13 = bf16[256,3,256]{2,0,1:T(8,128)(2,1)} collective-permute-done((bf16[256,3,256]{2,0,1:T(8,128)(2,1)S(1)}, bf16[256,3,256]{2,0,1:T(8,128)(2,1)}, u32[]{:S(2)}, u32[]{:S(2)}) %collective-permute-start.13) | collective-permute-done | bytes 393248 | tf_op jit(solution)/shard_map/ppermute | solution.py:285
  95.8 7.8 %collective-permute-done.3 = bf16[1024,320]{0,1:T(8,128)(2,1)} collective-permute-done((bf16[1024,320]{0,1:T(8,128)(2,1)}, bf16[1024,320]{0,1:T(8,128)(2,1)}, u32[]{:S(2)}, u32[]{:S(2)}) %collective-permute-start.3) | collective-permute-done | bytes 655392 | tf_op jit(solution)/shard_map/ppermute | solution.py:285
  131.6 6.0 fusion.126
  143.4 7.1 %gather_fusion.1 = bf16[12,512,512]{2,1,0:T(8,128)(2,1)} fusion(bf16[12,512,512]{2,1,0:T(8,128)(2,1)} %bitcast.292, s32[1024]{0:T(1024)} %pad_clamp_fusion.1), kind=kCustom, calls=%fused_computation.1 | custom fusion | bytes 12582960 | tf_op jit(solution)/shard_map/jit(_take)/gather | solution.py:456
  150.5 3.4 select_bitcast_fusion
  162.6 3.3 fusion.128
  171.7 3.8 fusion.5
  181.0 4.3 collective-permute-start.15
  193.6 4.5 fusion.130
  232.9 5.7 collective-permute-start.17
  238.6 3.9 copy.109
  263.1 4.0 convolution_bitcast_fusion
  272.6 5.1 fusion.14
  286.7 5.9 collective-permute-start.19
  302.9 3.9 copy.108
  310.2 4.3 convolution_bitcast_fusion.3
  314.5 5.2 collective-permute-done.20
  324.0 4.0 convolution_bitcast_fusion.2
  336.3 5.0 maximum_maximum_fusion
  341.3 7.0 %gather_fusion.3 = bf16[12,512,512]{2,1,0:T(8,128)(2,1)} fusion(bf16[12,512,512]{2,1,0:T(8,128)(2,1)} %bitcast.291, s32[1024]{0:T(1024)S(1)} %pad_clamp_fusion), kind=kCustom, calls=%fused_computation.3 | custom fusion | bytes 12582960 | tf_op jit(solution)/shard_map/jit(_take)/gather | solution.py:612
  349.2 4.5 select_convert_fusion
  364.9 6.7 %collective-permute-done.51 = bf16[3,512,1,1,128]{4,1,3,2,0:T(8,128)(2,1)S(1)} collective-permute-done((bf16[3,512,1,1,128]{4,1,3,2,0:T(8,128)(2,1)}, bf16[3,512,1,1,128]{4,1,3,2,0:T(8,128)(2,1)S(1)}, u32[]{:S(2)}, u32[]{:S(2)}) %collective-permute-start.51) | collective-permute-done | bytes 393248 | tf_op jit(solution)/shard_map/ppermute | solution.py:285
  376.6 8.0 %collective-permute-done.52 = bf16[3,256,128]{2,1,0:T(8,128)(2,1)S(1)} collective-permute-done((bf16[3,256,128]{2,1,0:T(8,128)(2,1)S(1)}, bf16[3,256,128]{2,1,0:T(8,128)(2,1)S(1)}, u32[]{:S(2)}, u32[]{:S(2)}) %collective-permute-start.52) | collective-permute-done | bytes 196640 | tf_op jit(solution)/shard_map/ppermute | solution.py:285
  385.0 3.8 collective-permute-done.46
  392.7 12.8 %collective-permute-done.47 = bf16[1024,160]{0,1:T(8,128)(2,1)S(1)} collective-permute-done((bf16[1024,160]{0,1:T(8,128)(2,1)S(1)}, bf16[1024,160]{0,1:T(8,128)(2,1)S(1)}, u32[]{:S(2)}, u32[]{:S(2)}) %collective-permute-start.47) | collective-permute-done | bytes 327712 | tf_op jit(solution)/shard_map/ppermute | solution.py:285
  412.0 4.4 collective-permute-done.48
  416.5 6.8 %collective-permute-done.27 = bf16[512,512]{1,0:T(8,128)(2,1)S(1)} collective-permute-done((bf16[512,512]{1,0:T(8,128)(2,1)S(1)}, bf16[512,512]{1,0:T(8,128)(2,1)S(1)}, u32[]{:S(2)}, u32[]{:S(2)}) %collective-permute-start.27) | collective-permute-done | bytes 524320 | tf_op jit(solution)/shard_map/ppermute | solution.py:285
  423.3 11.2 %collective-permute-done.33 = bf16[512,512]{1,0:T(8,128)(2,1)S(1)} collective-permute-done((bf16[512,512]{1,0:T(8,128)(2,1)S(1)}, bf16[512,512]{1,0:T(8,128)(2,1)S(1)}, u32[]{:S(2)}, u32[]{:S(2)}) %collective-permute-start.33) | collective-permute-done | bytes 524320 | tf_op jit(solution)/shard_map/ppermute | solution.py:285
  434.5 10.0 %collective-permute-done.39 = bf16[512,512]{1,0:T(8,128)(2,1)S(1)} collective-permute-done((bf16[512,512]{1,0:T(8,128)(2,1)S(1)}, bf16[512,512]{1,0:T(8,128)(2,1)S(1)}, u32[]{:S(2)}, u32[]{:S(2)}) %collective-permute-start.39) | collective-permute-done | bytes 524320 | tf_op jit(solution)/shard_map/ppermute | solution.py:285
  449.0 4.9 collective-permute-done.28
  454.2 7.2 %collective-permute-done.34 = bf16[256,512]{1,0:T(8,128)(2,1)S(1)} collective-permute-done((bf16[256,512]{1,0:T(8,128)(2,1)S(1)}, bf16[256,512]{1,0:T(8,128)(2,1)S(1)}, u32[]{:S(2)}, u32[]{:S(2)}) %collective-permute-start.34) | collective-permute-done | bytes 262176 | tf_op jit(solution)/shard_map/ppermute | solution.py:285
  472.6 7.5 %collective-permute-done.30 = bf16[128,512]{1,0:T(8,128)(2,1)S(1)} collective-permute-done((bf16[128,512]{1,0:T(8,128)(2,1)S(1)}, bf16[128,512]{1,0:T(8,128)(2,1)S(1)}, u32[]{:S(2)}, u32[]{:S(2)}) %collective-permute-start.30) | collective-permute-done | bytes 131104 | tf_op jit(solution)/shard_map/ppermute | solution.py:285
  492.0 4.2 collective-permute-done.32
  496.3 4.5 collective-permute-done.38
  514.6 3.4 pad_maximum_fusion.1.tall_ref
  518.0 7.6 %fusion.108.gram_ref = f32[6,512,512]{2,1,0:T(8,128)} fusion(f32[3,512,512]{2,1,0:T(8,128)S(1)} %fusion.132, f32[3,512,512]{2,1,0:T(8,128)S(1)} %fusion.131), kind=kOutput, calls=%fused_computation.321 | convolution fusion | flops 4833411072 | bytes 12582912 | tf_op jit(solution)/shard_map/dot_general | solution.py:229
  527.5 4.8 fusion.17
  532.4 5.3 fusion.31
  537.7 6.9 %fusion.133 = f32[3,512,512]{2,1,0:T(8,128)} fusion(f32[3,512,512]{2,1,0:T(8,128)S(1)} %fusion.31, f32[3,512,512]{2,1,0:T(8,128)S(1)} %copy-done.3), kind=kOutput, calls=%fused_computation.339 | convolution fusion | flops 2415919104 | bytes 9437184 | tf_op jit(solution)/shard_map/dot_general | solution.py:229
  544.6 59.8 %shard_map.401 = f32[6,512,512]{2,1,0:T(8,128)} custom-call(f32[6,512,512]{2,1,0:T(8,128)} %fusion.108.gram_ref, f32[6,512,512]{2,1,0:T(8,128)} %pad_maximum_fusion.1.tall_ref), custom_call_target="tpu_custom_call" | custom-call | tf_op jit(solution)/shard_map/pallas_call | solution.py:212
  604.4 7.1 %fusion.118 = (f32[3,512,512]{2,1,0:T(8,128)}, f32[3,512,512]{2,1,0:T(8,128)}) fusion(f32[6,512,512]{2,1,0:T(8,128)} %shard_map.401), kind=kLoop, calls=%fused_computation.324 | loop fusion | bytes 12582912 | tf_op jit(solution)/shard_map/slice | solution.py:278
  611.5 6.9 %fusion.135 = f32[3,512,512]{2,1,0:T(8,128)} fusion(f32[6,512,512]{2,1,0:T(8,128)S(1)} %copy-done.5, f32[3,512,512]{2,1,0:T(8,128)S(1)} %copy-done.52), kind=kOutput, calls=%fused_computation.341 | convolution fusion | flops 2415919104 | bytes 12582912 | tf_op jit(solution)/shard_map/dot_general | solution.py:229
  618.3 10.1 %multiply_subtract_fusion = f32[3,512,512]{2,1,0:T(8,128)} fusion(f32[3,512,512]{2,1,0:T(8,128)} %param.55, f32[3,512,512]{2,1,0:T(8,128)} %param.61, f32[3,512,512]{2,1,0:T(8,128)S(1)} %copy-done.2, f32[3,512,512]{2,1,0:T(8,128)} %get-tuple-element.291, f32[]{:T(128)} %bitcast.79, f32[]{:T(128)} %bitcast.78, f32[3,512,512]{2,1,0:T(8,128)} %copy-done.11, ...), kind=kOutput, calls=%fused_computation.35 | convolution fusion | flops 1622409216 | bytes 22020104 | tf_op jit(solution)/shard_map/dot_general | solution.py:235
  628.5 7.2 %fusion.134 = f32[3,512,512]{2,1,0:T(8,128)} fusion(f32[3,512,512]{2,1,0:T(8,128)} %fusion.135, f32[3,512,512]{2,1,0:T(8,128)} %get-tuple-element.203), kind=kOutput, calls=%fused_computation.340 | convolution fusion | flops 2415919104 | bytes 9437184 | tf_op jit(solution)/shard_map/dot_general | solution.py:229
  (568 shorter events, 268.5 us)
Async XLA Ops:
  4.1 122.0 %collective-permute-start.7 = (bf16[3,512,512]{2,1,0:T(8,128)(2,1)}, bf16[3,512,512]{2,1,0:T(8,128)(2,1)}, u32[]{:S(2)}, u32[]{:S(2)}) collective-permute-start(bf16[3,512,512]{2,1,0:T(8,128)(2,1)} %convert_element_type.95), channel_id=1, source_target_pairs={{0,2},{1,3},{2,0},{3,1},{4,6},{5,7},{6,4},{7,5},{8,10},{9,11},{10,... | collective-permute-start | bytes 4718600 | tf_op jit(solution)/shard_map/ppermute | solution.py:285
  7.0 119.3 %collective-permute-start.6 = (bf16[3,512,512]{2,1,0:T(8,128)(2,1)}, bf16[3,512,512]{2,1,0:T(8,128)(2,1)}, u32[]{:S(2)}, u32[]{:S(2)}) collective-permute-start(bf16[3,512,512]{2,1,0:T(8,128)(2,1)} %convert_element_type.95), channel_id=1, source_target_pairs={{0,1},{1,0},{2,3},{3,2},{4,5},{5,4},{6,7},{7,6},{8,9},{9,8},{10,11... | collective-permute-start | bytes 4718600 | tf_op jit(solution)/shard_map/ppermute | solution.py:285
  7.0 36.5 %collective-permute-start.10 = (bf16[64,3,128]{2,0,1:T(8,128)(2,1)S(1)}, bf16[64,3,128]{2,0,1:T(8,128)(2,1)S(1)}, u32[]{:S(2)}, u32[]{:S(2)}) collective-permute-start(bf16[64,3,128]{2,0,1:T(8,128)(2,1)S(1)} %convert_bitcast_fusion), channel_id=1, source_target_pairs={{0,2},{1,3},{2,0},{3,1},{4,6},{5,7},{6,4},{7,5},{8,10},{9,11},{10,... | collective-permute-start | bytes 147464 | tf_op jit(solution)/shard_map/ppermute | solution.py:285
  7.2 38.2 %collective-permute-start = (bf16[256,160]{0,1:T(8,128)(2,1)S(1)}, bf16[256,160]{0,1:T(8,128)(2,1)S(1)}, u32[]{:S(2)}, u32[]{:S(2)}) collective-permute-start(bf16[256,160]{0,1:T(8,128)(2,1)S(1)} %convert_element_type.93), channel_id=1, source_target_pairs={{0,2},{1,3},{2,0},{3,1},{4,6},{5,7},{6,4},{7,5},{8,10},{9,11},{10,... | collective-permute-start | bytes 245768 | tf_op jit(solution)/shard_map/ppermute | solution.py:285
  19.7 87.3 %collective-permute-start.5 = (bf16[2,64,512]{2,1,0:T(8,128)(2,1)}, bf16[2,64,512]{2,1,0:T(8,128)(2,1)}, u32[]{:S(2)}, u32[]{:S(2)}) collective-permute-start(bf16[2,64,512]{2,1,0:T(8,128)(2,1)} %get-tuple-element.245), channel_id=1, source_target_pairs={{0,4},{4,8},{8,12},{12,16},{16,20},{20,24},{24,28},{1,5},{5,9},{9,... | collective-permute-start | bytes 393224 | tf_op jit(solution)/shard_map/ppermute | solution.py:36
  49.3 12.1 %collective-permute-start.12 = (bf16[128,3,256]{2,0,1:T(8,128)(2,1)S(1)}, bf16[128,3,256]{2,0,1:T(8,128)(2,1)S(1)}, u32[]{:S(2)}, u32[]{:S(2)}) collective-permute-start(bf16[128,3,256]{2,0,1:T(8,128)(2,1)S(1)} %pad_maximum_fusion.32), channel_id=1, source_target_pairs={{0,8},{4,12},{8,0},{12,4},{16,24},{20,28},{24,16},{28,20},{1,9},{5... | collective-permute-start | bytes 589832 | tf_op jit(solution)/shard_map/ppermute | solution.py:285
  51.1 14.3 %collective-permute-start.2 = (bf16[512,320]{0,1:T(8,128)(2,1)S(1)}, bf16[512,320]{0,1:T(8,128)(2,1)S(1)}, u32[]{:S(2)}, u32[]{:S(2)}) collective-permute-start(bf16[512,320]{0,1:T(8,128)(2,1)S(1)} %pad_maximum_fusion.28), channel_id=1, source_target_pairs={{0,8},{4,12},{8,0},{12,4},{16,24},{20,28},{24,16},{28,20},{1,9},{5... | collective-permute-start | bytes 983048 | tf_op jit(solution)/shard_map/ppermute | solution.py:285
  61.5 32.1 %collective-permute-start.13 = (bf16[256,3,256]{2,0,1:T(8,128)(2,1)S(1)}, bf16[256,3,256]{2,0,1:T(8,128)(2,1)}, u32[]{:S(2)}, u32[]{:S(2)}) collective-permute-start(bf16[256,3,256]{2,0,1:T(8,128)(2,1)S(1)} %pad_maximum_fusion.27), channel_id=1, source_target_pairs={{0,16},{4,20},{8,24},{12,28},{16,0},{20,4},{24,8},{28,12},{1,17},{... | collective-permute-start | bytes 1179656 | tf_op jit(solution)/shard_map/ppermute | solution.py:285
  66.4 37.2 %collective-permute-start.3 = (bf16[1024,320]{0,1:T(8,128)(2,1)}, bf16[1024,320]{0,1:T(8,128)(2,1)}, u32[]{:S(2)}, u32[]{:S(2)}) collective-permute-start(bf16[1024,320]{0,1:T(8,128)(2,1)} %pad_maximum_fusion.18), channel_id=1, source_target_pairs={{0,16},{4,20},{8,24},{12,28},{16,0},{20,4},{24,8},{28,12},{1,17},{... | collective-permute-start | bytes 1966088 | tf_op jit(solution)/shard_map/ppermute | solution.py:285
  95.8 21.7 %collective-permute-start.14 = (bf16[512,3,256]{2,0,1:T(8,128)(2,1)}, bf16[512,3,256]{2,0,1:T(8,128)(2,1)}, u32[]{:S(2)}, u32[]{:S(2)}) collective-permute-start(bf16[512,3,256]{2,0,1:T(8,128)(2,1)} %pad_maximum_fusion.17), channel_id=1, source_target_pairs={{0,1},{1,0},{2,3},{3,2},{4,5},{5,4},{6,7},{7,6},{8,9},{9,8},{10,11... | collective-permute-start | bytes 2359304 | tf_op jit(solution)/shard_map/ppermute | solution.py:285
  107.0 21.3 %collective-permute-start.4 = (bf16[2048,320]{0,1:T(8,128)(2,1)}, bf16[2048,320]{0,1:T(8,128)(2,1)}, u32[]{:S(2)}, u32[]{:S(2)}) collective-permute-start(bf16[2048,320]{0,1:T(8,128)(2,1)} %pad_maximum_fusion.12), channel_id=1, source_target_pairs={{0,1},{1,0},{2,3},{3,2},{4,5},{5,4},{6,7},{7,6},{8,9},{9,8},{10,11... | collective-permute-start | bytes 3932168 | tf_op jit(solution)/shard_map/ppermute | solution.py:285
  107.0 8.0 %collective-permute-start.9 = (bf16[2,64,512]{2,1,0:T(8,128)(2,1)}, bf16[2,64,512]{2,1,0:T(8,128)(2,1)S(1)}, u32[]{:S(2)}, u32[]{:S(2)}) collective-permute-start(bf16[2,64,512]{2,1,0:T(8,128)(2,1)} %get-tuple-element.244), channel_id=1, source_target_pairs={{4,0},{8,4},{12,8},{16,12},{20,16},{24,20},{28,24},{5,1},{9,5},{13... | collective-permute-start | bytes 393224 | tf_op jit(solution)/shard_map/ppermute | solution.py:38
  126.1 11.6 %collective-permute-start.8 = (bf16[3,512,512]{2,1,0:T(8,128)(2,1)}, bf16[3,512,512]{2,1,0:T(8,128)(2,1)S(1)}, u32[]{:S(2)}, u32[]{:S(2)}) collective-permute-start(bf16[3,512,512]{2,1,0:T(8,128)(2,1)} %collective-permute-done.7), channel_id=1, source_target_pairs={{0,1},{1,0},{2,3},{3,2},{4,5},{5,4},{6,7},{7,6},{8,9},{9,8},{10,11... | collective-permute-start | bytes 4718600 | tf_op jit(solution)/shard_map/ppermute | solution.py:285
  181.0 21.9 %collective-permute-start.15 = (bf16[2,128,512]{2,1,0:T(8,128)(2,1)}, bf16[2,128,512]{2,1,0:T(8,128)(2,1)S(1)}, u32[]{:S(2)}, u32[]{:S(2)}) collective-permute-start(bf16[2,128,512]{2,1,0:T(8,128)(2,1)} %get-tuple-element.241), channel_id=1, source_target_pairs={{0,4},{4,8},{8,12},{12,16},{16,20},{20,24},{24,28},{1,5},{5,9},{9,... | collective-permute-start | bytes 786440 | tf_op jit(solution)/shard_map/ppermute | solution.py:36
  185.4 17.6 %collective-permute-start.16 = (bf16[2,128,512]{2,1,0:T(8,128)(2,1)S(1)}, bf16[2,128,512]{2,1,0:T(8,128)(2,1)S(1)}, u32[]{:S(2)}, u32[]{:S(2)}) collective-permute-start(bf16[2,128,512]{2,1,0:T(8,128)(2,1)S(1)} %get-tuple-element.240), channel_id=1, source_target_pairs={{4,0},{8,4},{12,8},{16,12},{20,16},{24,20},{28,24},{5,1},{9,5},{13... | collective-permute-start | bytes 786440 | tf_op jit(solution)/shard_map/ppermute | solution.py:38
  232.9 16.5 %collective-permute-start.17 = (f32[2,128,512]{2,1,0:T(8,128)}, f32[2,128,512]{2,1,0:T(8,128)}, u32[]{:S(2)}, u32[]{:S(2)}) collective-permute-start(f32[2,128,512]{2,1,0:T(8,128)} %slice.604), channel_id=1, source_target_pairs={{0,4},{4,8},{8,12},{12,16},{16,20},{20,24},{24,28},{1,5},{5,9},{9,... | collective-permute-start | bytes 1572872 | tf_op jit(solution)/shard_map/ppermute | solution.py:36
  251.6 15.9 %collective-permute-start.18 = (f32[2,128,512]{2,1,0:T(8,128)}, f32[2,128,512]{2,1,0:T(8,128)}, u32[]{:S(2)}, u32[]{:S(2)}) collective-permute-start(f32[2,128,512]{2,1,0:T(8,128)} %get-tuple-element.218), channel_id=1, source_target_pairs={{4,0},{8,4},{12,8},{16,12},{20,16},{24,20},{28,24},{5,1},{9,5},{13... | collective-permute-start | bytes 1572872 | tf_op jit(solution)/shard_map/ppermute | solution.py:38
  286.7 20.1 %collective-permute-start.19 = (f32[2,64,512]{2,1,0:T(8,128)}, f32[2,64,512]{2,1,0:T(8,128)}, u32[]{:S(2)}, u32[]{:S(2)}) collective-permute-start(f32[2,64,512]{2,1,0:T(8,128)} %slice.610), channel_id=1, source_target_pairs={{0,4},{4,8},{8,12},{12,16},{16,20},{20,24},{24,28},{1,5},{5,9},{9,... | collective-permute-start | bytes 786440 | tf_op jit(solution)/shard_map/ppermute | solution.py:36
  299.6 59.1 %collective-permute-start.50 = (bf16[3,512,2,1,128]{4,1,3,2,0:T(8,128)(2,1)}, bf16[3,512,2,1,128]{4,1,3,2,0:T(8,128)(2,1)}, u32[]{:S(2)}, u32[]{:S(2)}) collective-permute-start(bf16[3,512,2,1,128]{4,1,3,2,0:T(8,128)(2,1)} %constant_dynamic-slice_fusion.4), channel_id=1, source_target_pairs={{0,1},{1,0},{2,3},{3,2},{4,5},{5,4},{6,7},{7,6},{8,9},{9,8},{10,11... | collective-permute-start | bytes 2359304 | tf_op jit(solution)/shard_map/ppermute | solution.py:285
  300.8 70.9 %collective-permute-start.45 = (bf16[2048,2,1,160]{0,3,2,1:T(8,128)(2,1)}, bf16[2048,2,1,160]{0,3,2,1:T(8,128)(2,1)}, u32[]{:S(2)}, u32[]{:S(2)}) collective-permute-start(bf16[2048,2,1,160]{0,3,2,1:T(8,128)(2,1)} %constant_dynamic-slice_fusion.8), channel_id=1, source_target_pairs={{0,1},{1,0},{2,3},{3,2},{4,5},{5,4},{6,7},{7,6},{8,9},{9,8},{10,11... | collective-permute-start | bytes 3932168 | tf_op jit(solution)/shard_map/ppermute | solution.py:285
  308.7 11.0 %collective-permute-start.20 = (f32[2,64,512]{2,1,0:T(8,128)S(1)}, f32[2,64,512]{2,1,0:T(8,128)S(1)}, u32[]{:S(2)}, u32[]{:S(2)}) collective-permute-start(f32[2,64,512]{2,1,0:T(8,128)S(1)} %get-tuple-element.224), channel_id=1, source_target_pairs={{4,0},{8,4},{12,8},{16,12},{20,16},{24,20},{28,24},{5,1},{9,5},{13... | collective-permute-start | bytes 786440 | tf_op jit(solution)/shard_map/ppermute | solution.py:38
  333.6 14.7 %collective-permute-start.23 = (f32[72,128]{1,0:T(8,128)S(1)}, f32[72,128]{1,0:T(8,128)S(1)}, u32[]{:S(2)}, u32[]{:S(2)}) collective-permute-start(f32[72,128]{1,0:T(8,128)S(1)} %fusion.197), channel_id=1, source_target_pairs={{0,4},{4,0},{8,12},{12,8},{16,20},{20,16},{24,28},{28,24},{1,5},{5... | collective-permute-start | bytes 110600 | tf_op jit(solution)/shard_map/ppermute | solution.py:285
  357.3 48.3 %collective-permute-start.26 = (bf16[2,1,3,512,512]{4,3,2,1,0:T(8,128)(2,1)}, bf16[2,1,3,512,512]{4,3,2,1,0:T(8,128)(2,1)}, u32[]{:S(2)}, u32[]{:S(2)}) collective-permute-start(bf16[2,1,3,512,512]{4,3,2,1,0:T(8,128)(2,1)} %constant_dynamic-slice_fusion.15), channel_id=1, source_target_pairs={{0,1},{1,0},{2,3},{3,2},{4,5},{5,4},{6,7},{7,6},{8,9},{9,8},{10,11... | collective-permute-start | bytes 9437192 | tf_op jit(solution)/shard_map/ppermute | solution.py:285
  361.2 10.5 %collective-permute-start.51 = (bf16[3,512,1,1,128]{4,1,3,2,0:T(8,128)(2,1)}, bf16[3,512,1,1,128]{4,1,3,2,0:T(8,128)(2,1)S(1)}, u32[]{:S(2)}, u32[]{:S(2)}) collective-permute-start(bf16[3,512,1,1,128]{4,1,3,2,0:T(8,128)(2,1)} %constant_dynamic-slice_fusion.3), channel_id=1, source_target_pairs={{0,2},{1,3},{2,0},{3,1},{4,6},{5,7},{6,4},{7,5},{8,10},{9,11},{10,... | collective-permute-start | bytes 1179656 | tf_op jit(solution)/shard_map/ppermute | solution.py:285
  373.8 15.1 %collective-permute-start.46 = (bf16[2048,1,1,160]{0,3,2,1:T(8,128)(2,1)S(1)}, bf16[2048,1,1,160]{0,3,2,1:T(8,128)(2,1)S(1)}, u32[]{:S(2)}, u32[]{:S(2)}) collective-permute-start(bf16[2048,1,1,160]{0,3,2,1:T(8,128)(2,1)S(1)} %constant_dynamic-slice_fusion.7), channel_id=1, source_target_pairs={{0,2},{1,3},{2,0},{3,1},{4,6},{5,7},{6,4},{7,5},{8,10},{9,11},{10,... | collective-permute-start | bytes 1966088 | tf_op jit(solution)/shard_map/ppermute | solution.py:285
  374.4 10.2 %collective-permute-start.52 = (bf16[3,256,128]{2,1,0:T(8,128)(2,1)S(1)}, bf16[3,256,128]{2,1,0:T(8,128)(2,1)S(1)}, u32[]{:S(2)}, u32[]{:S(2)}) collective-permute-start(bf16[3,256,128]{2,1,0:T(8,128)(2,1)S(1)} %dynamic-slice_bitcast_fusion.3), channel_id=1, source_target_pairs={{0,16},{4,20},{8,24},{12,28},{16,0},{20,4},{24,8},{28,12},{1,17},{... | collective-permute-start | bytes 589832 | tf_op jit(solution)/shard_map/ppermute | solution.py:285
  384.7 7.1 %collective-permute-start.53 = (bf16[3,128,128]{2,1,0:T(8,128)(2,1)S(1)}, bf16[3,128,128]{2,1,0:T(8,128)(2,1)S(1)}, u32[]{:S(2)}, u32[]{:S(2)}) collective-permute-start(bf16[3,128,128]{2,1,0:T(8,128)(2,1)S(1)} %constant_dynamic-slice_fusion.2), channel_id=1, source_target_pairs={{0,8},{4,12},{8,0},{12,4},{16,24},{20,28},{24,16},{28,20},{1,9},{5... | collective-permute-start | bytes 294920 | tf_op jit(solution)/shard_map/ppermute | solution.py:285
  389.0 16.5 %collective-permute-start.47 = (bf16[1024,160]{0,1:T(8,128)(2,1)S(1)}, bf16[1024,160]{0,1:T(8,128)(2,1)S(1)}, u32[]{:S(2)}, u32[]{:S(2)}) collective-permute-start(bf16[1024,160]{0,1:T(8,128)(2,1)S(1)} %dynamic-slice_bitcast_fusion.2), channel_id=1, source_target_pairs={{0,16},{4,20},{8,24},{12,28},{16,0},{20,4},{24,8},{28,12},{1,17},{... | collective-permute-start | bytes 983048 | tf_op jit(solution)/shard_map/ppermute | solution.py:285
  391.9 19.4 %collective-permute-start.54 = (bf16[3,64,128]{2,1,0:T(8,128)(2,1)S(1)}, bf16[3,64,128]{2,1,0:T(8,128)(2,1)S(1)}, u32[]{:S(2)}, u32[]{:S(2)}) collective-permute-start(bf16[3,64,128]{2,1,0:T(8,128)(2,1)S(1)} %constant_dynamic-slice_fusion.1), channel_id=1, source_target_pairs={{0,4},{4,0},{8,12},{12,8},{16,20},{20,16},{24,28},{28,24},{1,5},{5... | collective-permute-start | bytes 147464 | tf_op jit(solution)/shard_map/ppermute | solution.py:285
  408.4 14.9 %collective-permute-start.27 = (bf16[512,512]{1,0:T(8,128)(2,1)S(1)}, bf16[512,512]{1,0:T(8,128)(2,1)S(1)}, u32[]{:S(2)}, u32[]{:S(2)}) collective-permute-start(bf16[512,512]{1,0:T(8,128)(2,1)S(1)} %get-tuple-element.231), channel_id=1, source_target_pairs={{0,2},{1,3},{2,0},{3,1},{4,6},{5,7},{6,4},{7,5},{8,10},{9,11},{10,... | collective-permute-start | bytes 1572872 | tf_op jit(solution)/shard_map/ppermute | solution.py:285
  409.0 25.5 %collective-permute-start.33 = (bf16[512,512]{1,0:T(8,128)(2,1)S(1)}, bf16[512,512]{1,0:T(8,128)(2,1)S(1)}, u32[]{:S(2)}, u32[]{:S(2)}) collective-permute-start(bf16[512,512]{1,0:T(8,128)(2,1)S(1)} %get-tuple-element.233), channel_id=1, source_target_pairs={{0,2},{1,3},{2,0},{3,1},{4,6},{5,7},{6,4},{7,5},{8,10},{9,11},{10,... | collective-permute-start | bytes 1572872 | tf_op jit(solution)/shard_map/ppermute | solution.py:285
  410.5 34.0 %collective-permute-start.39 = (bf16[512,512]{1,0:T(8,128)(2,1)S(1)}, bf16[512,512]{1,0:T(8,128)(2,1)S(1)}, u32[]{:S(2)}, u32[]{:S(2)}) collective-permute-start(bf16[512,512]{1,0:T(8,128)(2,1)S(1)} %get-tuple-element.232), channel_id=1, source_target_pairs={{0,2},{1,3},{2,0},{3,1},{4,6},{5,7},{6,4},{7,5},{8,10},{9,11},{10,... | collective-permute-start | bytes 1572872 | tf_op jit(solution)/shard_map/ppermute | solution.py:285
  444.7 9.2 %collective-permute-start.28 = (bf16[256,512]{1,0:T(8,128)(2,1)S(1)}, bf16[256,512]{1,0:T(8,128)(2,1)S(1)}, u32[]{:S(2)}, u32[]{:S(2)}) collective-permute-start(bf16[256,512]{1,0:T(8,128)(2,1)S(1)} %constant_dynamic-slice_fusion.14), channel_id=1, source_target_pairs={{0,4},{4,0},{8,12},{12,8},{16,20},{20,16},{24,28},{28,24},{1,5},{5... | collective-permute-start | bytes 786440 | tf_op jit(solution)/shard_map/ppermute | solution.py:285
  445.5 34.7 %collective-permute-start.49 = (bf16[256,160]{0,1:T(8,128)(2,1)S(1)}, bf16[256,160]{0,1:T(8,128)(2,1)S(1)}, u32[]{:S(2)}, u32[]{:S(2)}) collective-permute-start(bf16[256,160]{0,1:T(8,128)(2,1)S(1)} %constant_dynamic-slice_fusion.5), channel_id=1, source_target_pairs={{0,4},{4,0},{8,12},{12,8},{16,20},{20,16},{24,28},{28,24},{1,5},{5... | collective-permute-start | bytes 245768 | tf_op jit(solution)/shard_map/ppermute | solution.py:285
  446.8 14.5 %collective-permute-start.34 = (bf16[256,512]{1,0:T(8,128)(2,1)S(1)}, bf16[256,512]{1,0:T(8,128)(2,1)S(1)}, u32[]{:S(2)}, u32[]{:S(2)}) collective-permute-start(bf16[256,512]{1,0:T(8,128)(2,1)S(1)} %constant_dynamic-slice_fusion.12), channel_id=1, source_target_pairs={{0,4},{4,0},{8,12},{12,8},{16,20},{20,16},{24,28},{28,24},{1,5},{5... | collective-permute-start | bytes 786440 | tf_op jit(solution)/shard_map/ppermute | solution.py:285
  447.7 17.2 %collective-permute-start.40 = (bf16[256,512]{1,0:T(8,128)(2,1)S(1)}, bf16[256,512]{1,0:T(8,128)(2,1)S(1)}, u32[]{:S(2)}, u32[]{:S(2)}) collective-permute-start(bf16[256,512]{1,0:T(8,128)(2,1)S(1)} %constant_dynamic-slice_fusion.10), channel_id=1, source_target_pairs={{0,4},{4,0},{8,12},{12,8},{16,20},{20,16},{24,28},{28,24},{1,5},{5... | collective-permute-start | bytes 786440 | tf_op jit(solution)/shard_map/ppermute | solution.py:285
  454.1 11.0 %collective-permute-start.29 = (bf16[128,512]{1,0:T(8,128)(2,1)S(1)}, bf16[128,512]{1,0:T(8,128)(2,1)S(1)}, u32[]{:S(2)}, u32[]{:S(2)}) collective-permute-start(bf16[128,512]{1,0:T(8,128)(2,1)S(1)} %constant_dynamic-slice_fusion.13), channel_id=1, source_target_pairs={{0,8},{4,12},{8,0},{12,4},{16,24},{20,28},{24,16},{28,20},{1,9},{5... | collective-permute-start | bytes 393224 | tf_op jit(solution)/shard_map/ppermute | solution.py:285
  461.4 7.3 %collective-permute-start.35 = (bf16[128,512]{1,0:T(8,128)(2,1)S(1)}, bf16[128,512]{1,0:T(8,128)(2,1)S(1)}, u32[]{:S(2)}, u32[]{:S(2)}) collective-permute-start(bf16[128,512]{1,0:T(8,128)(2,1)S(1)} %constant_dynamic-slice_fusion.11), channel_id=1, source_target_pairs={{0,8},{4,12},{8,0},{12,4},{16,24},{20,28},{24,16},{28,20},{1,9},{5... | collective-permute-start | bytes 393224 | tf_op jit(solution)/shard_map/ppermute | solution.py:285
  464.9 7.2 %collective-permute-start.41 = (bf16[128,512]{1,0:T(8,128)(2,1)S(1)}, bf16[128,512]{1,0:T(8,128)(2,1)S(1)}, u32[]{:S(2)}, u32[]{:S(2)}) collective-permute-start(bf16[128,512]{1,0:T(8,128)(2,1)S(1)} %constant_dynamic-slice_fusion.9), channel_id=1, source_target_pairs={{0,8},{4,12},{8,0},{12,4},{16,24},{20,28},{24,16},{28,20},{1,9},{5... | collective-permute-start | bytes 393224 | tf_op jit(solution)/shard_map/ppermute | solution.py:285
  465.1 15.0 %collective-permute-start.30 = (bf16[128,512]{1,0:T(8,128)(2,1)S(1)}, bf16[128,512]{1,0:T(8,128)(2,1)S(1)}, u32[]{:S(2)}, u32[]{:S(2)}) collective-permute-start(bf16[128,512]{1,0:T(8,128)(2,1)S(1)} %dynamic-slice_add_fusion.11), channel_id=1, source_target_pairs={{0,16},{4,20},{8,24},{12,28},{16,0},{20,4},{24,8},{28,12},{1,17},{... | collective-permute-start | bytes 393224 | tf_op jit(solution)/shard_map/ppermute | solution.py:285
  468.8 13.9 %collective-permute-start.36 = (bf16[128,512]{1,0:T(8,128)(2,1)S(1)}, bf16[128,512]{1,0:T(8,128)(2,1)S(1)}, u32[]{:S(2)}, u32[]{:S(2)}) collective-permute-start(bf16[128,512]{1,0:T(8,128)(2,1)S(1)} %dynamic-slice_add_fusion.10), channel_id=1, source_target_pairs={{0,16},{4,20},{8,24},{12,28},{16,0},{20,4},{24,8},{28,12},{1,17},{... | collective-permute-start | bytes 393224 | tf_op jit(solution)/shard_map/ppermute | solution.py:285
  472.1 11.9 %collective-permute-start.42 = (bf16[128,512]{1,0:T(8,128)(2,1)S(1)}, bf16[128,512]{1,0:T(8,128)(2,1)S(1)}, u32[]{:S(2)}, u32[]{:S(2)}) collective-permute-start(bf16[128,512]{1,0:T(8,128)(2,1)S(1)} %dynamic-slice_add_fusion.9), channel_id=1, source_target_pairs={{0,16},{4,20},{8,24},{12,28},{16,0},{20,4},{24,8},{28,12},{1,17},{... | collective-permute-start | bytes 393224 | tf_op jit(solution)/shard_map/ppermute | solution.py:285
  480.1 6.7 %collective-permute-start.31 = (bf16[128,512]{1,0:T(8,128)(2,1)S(1)}, bf16[128,512]{1,0:T(8,128)(2,1)S(1)}, u32[]{:S(2)}, u32[]{:S(2)}) collective-permute-start(bf16[128,512]{1,0:T(8,128)(2,1)S(1)} %add.604), channel_id=1, source_target_pairs={{0,8},{4,12},{8,0},{12,4},{16,24},{20,28},{24,16},{28,20},{1,9},{5... | collective-permute-start | bytes 393224 | tf_op jit(solution)/shard_map/ppermute | solution.py:285
  482.7 6.9 %collective-permute-start.37 = (bf16[128,512]{1,0:T(8,128)(2,1)S(1)}, bf16[128,512]{1,0:T(8,128)(2,1)S(1)}, u32[]{:S(2)}, u32[]{:S(2)}) collective-permute-start(bf16[128,512]{1,0:T(8,128)(2,1)S(1)} %add.608), channel_id=1, source_target_pairs={{0,8},{4,12},{8,0},{12,4},{16,24},{20,28},{24,16},{28,20},{1,9},{5... | collective-permute-start | bytes 393224 | tf_op jit(solution)/shard_map/ppermute | solution.py:285
  484.1 6.9 %collective-permute-start.43 = (bf16[128,512]{1,0:T(8,128)(2,1)S(1)}, bf16[128,512]{1,0:T(8,128)(2,1)S(1)}, u32[]{:S(2)}, u32[]{:S(2)}) collective-permute-start(bf16[128,512]{1,0:T(8,128)(2,1)S(1)} %add.612), channel_id=1, source_target_pairs={{0,8},{4,12},{8,0},{12,4},{16,24},{20,28},{24,16},{28,20},{1,9},{5... | collective-permute-start | bytes 393224 | tf_op jit(solution)/shard_map/ppermute | solution.py:285
  486.9 9.2 %collective-permute-start.32 = (bf16[256,512]{1,0:T(8,128)(2,1)S(1)}, bf16[256,512]{1,0:T(8,128)(2,1)S(1)}, u32[]{:S(2)}, u32[]{:S(2)}) collective-permute-start(bf16[256,512]{1,0:T(8,128)(2,1)S(1)} %pad_maximum_fusion.29), channel_id=1, source_target_pairs={{0,4},{4,0},{8,12},{12,8},{16,20},{20,16},{24,28},{28,24},{1,5},{5... | collective-permute-start | bytes 786440 | tf_op jit(solution)/shard_map/ppermute | solution.py:285
  489.7 11.1 %collective-permute-start.38 = (bf16[256,512]{1,0:T(8,128)(2,1)S(1)}, bf16[256,512]{1,0:T(8,128)(2,1)S(1)}, u32[]{:S(2)}, u32[]{:S(2)}) collective-permute-start(bf16[256,512]{1,0:T(8,128)(2,1)S(1)} %pad_maximum_fusion.30), channel_id=1, source_target_pairs={{0,4},{4,0},{8,12},{12,8},{16,20},{20,16},{24,28},{28,24},{1,5},{5... | collective-permute-start | bytes 786440 | tf_op jit(solution)/shard_map/ppermute | solution.py:285
  491.1 12.5 %collective-permute-start.44 = (bf16[256,512]{1,0:T(8,128)(2,1)S(1)}, bf16[256,512]{1,0:T(8,128)(2,1)S(1)}, u32[]{:S(2)}, u32[]{:S(2)}) collective-permute-start(bf16[256,512]{1,0:T(8,128)(2,1)S(1)} %pad_maximum_fusion.31), channel_id=1, source_target_pairs={{0,4},{4,0},{8,12},{12,8},{16,20},{20,16},{24,28},{28,24},{1,5},{5... | collective-permute-start | bytes 786440 | tf_op jit(solution)/shard_map/ppermute | solution.py:285
  (127 other events, 912.2 us)
